TPU v7x, 256 devices: a whole 4x4x8 slice. The times are simulated.
256 devices in a mesh: gx: 4 (over x), gy: 4 (over y), gz: 16 (over z, core).
Axes of the slice: x: 4, y: 4, z: 8, core: 2. Of those that a mesh axis runs over, the one named last changes fastest.
Arguments:
- incidence: int32 [4, 4, 16, 16, 16, 8, 128], P('gx', 'gy', 'gz'), may hold values from 0 to 1, as said below
- live_counts: int32 [4, 4, 16, 16], P('gx', 'gy', 'gz'), may hold values from 1 to 16, as said below
- lame_first: float32 [4, 4, 16, 16, 16], P('gx', 'gy', 'gz'), may hold values from 0.5 to 2
- shear_modulus: float32 [4, 4, 16, 16, 16], P('gx', 'gy', 'gz'), may hold values from 0.5 to 4.5
- stretch: float32 [3, 4, 4, 16, 16, 16], P(None, 'gx', 'gy', 'gz'), may hold values from 0.5 to 2
Outputs:
- stiffness: float32 [4, 4, 16, 3, 128, 3, 128], P('gx', 'gy', 'gz')
Inputs may be any that keep to these rules, and one draw needn't show every extreme that they name: `incidence`: each element slot names 8 distinct nodes of the tile, some corners replaced by all-zero rows; corner 0 of every slot is always present. `live_counts`: among the 16 tiles of one element block and one node block, at least one has exactly 16 live slots.
All inputs are finite; a program needn't handle non-finite values.
Results may differ from a plain program's by a relative error of at most 0.000059.
Values sent between devices are 32-bit elements; how exact they have to be, the bound alone decides.
A program may use at most 64 MiB of HBM per device.

v0:
```python
import functools
import math

import jax
import jax.numpy as jnp
import numpy as np
from jax import lax
from jax.sharding import Mesh
from jax.sharding import PartitionSpec as P

GZ = ("gz_0", "gz_1")
GX_GY_GZ = ("gx", "gy", "gz_0", "gz_1")


def over_axes(shard, axes):
    return functools.reduce(lax.psum, axes, shard)


def corner_table():
    corner_signs = np.array(
        [
            [sign_x, sign_y, sign_z]
            for sign_z in (-1.0, 1.0)
            for sign_y in (-1.0, 1.0)
            for sign_x in (-1.0, 1.0)
        ]
    )
    gauss_points = corner_signs / math.sqrt(3.0)
    shape_grads = np.zeros((8, 8, 3))
    for gauss_index in range(8):
        for corner_index in range(8):
            for axis_index in range(3):
                product_value = corner_signs[corner_index, axis_index] / 8.0
                for other_axis in range(3):
                    if other_axis != axis_index:
                        product_value = product_value * (
                            1.0
                            + corner_signs[corner_index, other_axis]
                            * gauss_points[gauss_index, other_axis]
                        )
                shape_grads[gauss_index, corner_index, axis_index] = product_value
    table_values = np.zeros((8, 3, 8, 3))
    for gauss_index in range(8):
        for first_corner in range(8):
            for first_axis in range(3):
                for second_corner in range(8):
                    for second_axis in range(3):
                        table_values[first_corner, first_axis, second_corner, second_axis] += (
                            shape_grads[gauss_index, first_corner, first_axis]
                            * shape_grads[gauss_index, second_corner, second_axis]
                        )
    return table_values


def element_matrices(first_param, shear_values, lengths):
    inverse = 2.0 / lengths
    scaling = inverse[:, None, :] * inverse[None, :, :]
    volume = lengths[0] * lengths[1] * lengths[2] / 8.0
    ref_table = jnp.asarray(corner_table(), jnp.float32)
    coupled = ref_table[None] * jnp.transpose(scaling, (2, 0, 1))[:, None, :, None, :]
    contracted = coupled[:, :, 0, :, 0] + coupled[:, :, 1, :, 1] + coupled[:, :, 2, :, 2]
    unit_matrix = jnp.eye(3, dtype=jnp.float32)
    matrices = first_param[:, None, None, None, None] * coupled + shear_values[
        :, None, None, None, None
    ] * (
        contracted[:, :, None, :, None] * unit_matrix[None, None, :, None, :]
        + jnp.transpose(coupled, (0, 1, 4, 3, 2))
    )
    return matrices * volume[:, None, None, None, None]


def assemble_block(matrices, onehot):
    spread = jnp.einsum("epiqj,eqb->epijb", matrices, onehot, precision=lax.Precision.HIGHEST)
    return jnp.einsum("epa,epijb->iajb", onehot, spread, precision=lax.Precision.HIGHEST)


def on_device(incidence, live_counts, lame_first, shear_modulus, stretch):
    local_tiles = incidence.shape[3]
    capacity = incidence.shape[4]
    tile_width = incidence.shape[6]
    onehot = incidence.reshape(local_tiles, capacity, 8, tile_width)
    alive_mask = jnp.arange(capacity, dtype=jnp.int32)[None, :] < live_counts.reshape(
        local_tiles, 1
    )
    first_param = lame_first.reshape(local_tiles, capacity)
    shear_values = shear_modulus.reshape(local_tiles, capacity)
    lengths = stretch.reshape(3, local_tiles, capacity)
    node_iota = lax.broadcasted_iota(jnp.int32, onehot.shape, 3)
    present = jnp.sum(onehot, axis=3) > 0
    position = jnp.sum(onehot * node_iota, axis=3)
    node_ids = jnp.where(present & alive_mask[:, :, None], position, -1)
    params = jnp.stack([first_param, shear_values, lengths[0], lengths[1], lengths[2]], axis=2)
    params = lax.all_to_all(params, GZ, split_axis=0, concat_axis=0, tiled=True)
    node_ids = lax.all_to_all(node_ids, GZ, split_axis=0, concat_axis=0, tiled=True)
    node_range = jnp.arange(tile_width, dtype=jnp.int32)

    def add_source(accumulated, packed):
        source_params, source_nodes = packed
        matrices = element_matrices(
            source_params[:, 0], source_params[:, 1], source_params[:, 2:].T
        )
        spread_onehot = (source_nodes[:, :, None] == node_range).astype(jnp.float32)
        return (accumulated + assemble_block(matrices, spread_onehot), None)

    initial = jnp.zeros((3, tile_width, 3, tile_width), jnp.float32)
    tile_block, unused = lax.scan(add_source, initial, (params, node_ids))
    tile_block = tile_block[None]
    diag_sum = jnp.trace(tile_block.reshape(3 * tile_width, 3 * tile_width))
    grand_total = over_axes(diag_sum, GX_GY_GZ)
    tile_count = lax.axis_size("gx") * lax.axis_size("gy") * local_tiles
    mean_diag = grand_total / (3 * tile_width * tile_count)
    return (tile_block / mean_diag).reshape(1, 1, 1, 3, tile_width, 3, tile_width)


def solution(mesh):
    finer = Mesh(
        mesh.devices.reshape(mesh.shape["gx"], mesh.shape["gy"], 8, 2), ("gx", "gy", "gz_0", "gz_1")
    )
    in_specs = (
        P("gx", "gy", GZ, None, None, None, None),
        P("gx", "gy", GZ, None),
        P("gx", "gy", GZ, None, None),
        P("gx", "gy", GZ, None, None),
        P(None, "gx", "gy", GZ, None, None),
    )
    out_specs = P("gx", "gy", GZ, None, None, None, None)
    return jax.shard_map(
        on_device, mesh=finer, in_specs=in_specs, out_specs=out_specs, check_vma=False
    )
```

profile of v0, /device:TPU:1, one launch (start us, length us, event | category | flops | bytes accessed | tf_op | source)
XLA Modules:
  0.0 122.8 jit_solution(3035923612780013202)
XLA Ops:
  0.0 5.7 %fusion.13 = s32[16,16,8]{2,1,0:T(8,128)S(1)} fusion(s32[1,1,1,16,16,8,128]{6,5,4,3,2,1,0:T(8,128)} %param.8), kind=kLoop, calls=%fused_computation.26 | loop fusion | flops 522240 | bytes 1056768 | tf_op jit(solution)/shard_map/reduce_sum | solution.py:90
  5.7 4.4 %reduce_sum.28 = s32[16,16,8]{2,1,0:T(8,128)S(1)} reduce(s32[1,1,1,16,16,8,128]{6,5,4,3,2,1,0:T(8,128)S(1)} %copy-done.1, s32[]{:T(128)} %constant.28.clone.1), dimensions={0,1,2,6}, to_apply=%region_0.0 | reduce | flops 260096 | bytes 1056772 | tf_op jit(solution)/shard_map/reduce_sum | solution.py:89
  11.0 0.7 reshape.102
  11.7 10.0 %all-to-all-start.1 = ((s32[16,1,128]{2,1,0:T(1,128)}), s32[16,1,128]{2,1,0:T(1,128)S(1)}, u32[]{:S(2)}, u32[]{:S(2)}) async-start(s32[16,1,128]{2,1,0:T(1,128)} %reshape.102), calls=%async_computation.1 | async-start | bytes 16384 | tf_op jit(solution)/shard_map/all_to_all | solution.py:94
  22.4 0.7 stack.3
  23.1 5.6 %all-to-all-done.1 = s32[16,1,128]{2,1,0:T(1,128)S(1)} async-done(((s32[16,1,128]{2,1,0:T(1,128)}), s32[16,1,128]{2,1,0:T(1,128)S(1)}, u32[]{:S(2)}, u32[]{:S(2)}) %all-to-all-start.1) | async-done | bytes 8224 | tf_op jit(solution)/shard_map/all_to_all | solution.py:94
  28.8 3.9 %all-to-all-start = ((f32[16,16,5]{1,2,0:T(8,128)}), f32[16,16,5]{1,2,0:T(8,128)S(1)}, u32[]{:S(2)}, u32[]{:S(2)}) async-start(f32[16,16,5]{1,2,0:T(8,128)} %stack.3), calls=%async_computation | async-start | bytes 131072 | tf_op jit(solution)/shard_map/all_to_all | solution.py:93
  33.9 6.6 %all-to-all-done = f32[16,16,5]{1,2,0:T(8,128)S(1)} async-done(((f32[16,16,5]{1,2,0:T(8,128)}), f32[16,16,5]{1,2,0:T(8,128)S(1)}, u32[]{:S(2)}, u32[]{:S(2)}) %all-to-all-start) | async-done | bytes 5152 | tf_op jit(solution)/shard_map/all_to_all | solution.py:93
  40.5 38.9 %while.12 = (s32[]{:T(128)}, f32[3,128,3,128]{1,3,0,2:T(8,128)S(1)}, f32[16,16,5]{1,2,0:T(8,128)S(1)}, s32[16,16,8]{1,2,0:T(8,128)S(1)}, s32[]{:T(128)}, /*index...) while((s32[]{:T(128)}, f32[3,128,3,128]{1,3,0,2:T(8,128)S(1)}, ...), condition=%wide.region_3.4_spmd.clone.clone, body=%wide.region_2.3_spmd.sunk.clone.clone.sunk | while | flops 241061120 | bytes 3757743 | solution.py:106
  42.0 0.7 fusion.31
  43.8 0.7 fusion.30
  44.5 0.7 fusion.31
  46.9 0.7 fusion.31
  49.3 0.7 fusion.31
  51.8 0.7 fusion.31
  54.2 0.7 fusion.31
  56.7 0.7 fusion.31
  59.1 0.7 fusion.31
  61.5 0.7 fusion.31
  64.0 0.7 fusion.31
  66.4 0.7 fusion.31
  68.8 0.7 fusion.31
  71.3 0.7 fusion.31
  73.7 0.7 fusion.31
  76.1 0.7 fusion.31
  78.6 0.7 fusion.31
  79.5 0.8 select_reduce_fusion
  80.3 9.1 %psum.28 = f32[]{:T(128)} all-reduce(f32[]{:T(128)} %select_reduce_fusion), channel_id=1, replica_groups=mesh['gx'=4,'gy'=4,'gz_0'=8,'gz_1'=2] {'gx'}, use_global_device_ids=true, to_apply=%region_5.6 | all-reduce | flops 1 | bytes 8 | tf_op jit(solution)/shard_map/psum | solution.py:16
  89.4 9.3 %psum.29 = f32[]{:T(128)} all-reduce(f32[]{:T(128)} %psum.28), channel_id=1, replica_groups=mesh['gx'=4,'gy'=4,'gz_0'=8,'gz_1'=2] {'gy'}, use_global_device_ids=true, to_apply=%region_6.7 | all-reduce | flops 1 | bytes 8 | tf_op jit(solution)/shard_map/psum | solution.py:16
  98.7 11.5 %psum.30 = f32[]{:T(128)} all-reduce(f32[]{:T(128)} %psum.29), channel_id=1, replica_groups=mesh['gx'=4,'gy'=4,'gz_0'=8,'gz_1'=2] {'gz_0'}, use_global_device_ids=true, to_apply=%region_7.8 | all-reduce | flops 1 | bytes 8 | tf_op jit(solution)/shard_map/psum | solution.py:16
  110.5 10.8 %psum.31 = f32[]{:T(128)} all-reduce(f32[]{:T(128)} %psum.30), channel_id=1, replica_groups=mesh['gx'=4,'gy'=4,'gz_0'=8,'gz_1'=2] {'gz_1'}, use_global_device_ids=true, to_apply=%region_8.9 | all-reduce | flops 1 | bytes 8 | tf_op jit(solution)/shard_map/psum | solution.py:16
  121.9 0.9 divide_bitcast_fusion
  (247 shorter events, 28.6 us)
Async XLA Ops:
  0.0 5.7 %copy-start.1 = (s32[1,1,1,16,16,8,128]{6,5,4,3,2,1,0:T(8,128)S(1)}, s32[1,1,1,16,16,8,128]{6,5,4,3,2,1,0:T(8,128)}, u32[]{:S(2)}) copy-start(s32[1,1,1,16,16,8,128]{6,5,4,3,2,1,0:T(8,128)} %param.8) | copy-start | bytes 3145732
  10.1 0.7 copy-start.6
  11.0 10.7 %copy-start.3 = (f32[3,1,1,1,16,16]{5,4,3,2,1,0:T(8,128)S(1)}, f32[3,1,1,1,16,16]{5,4,3,2,1,0:T(8,128)}, u32[]{:S(2)}) copy-start(f32[3,1,1,1,16,16]{5,4,3,2,1,0:T(8,128)} %param.12) | copy-start | bytes 9220
  11.7 17.0 %all-to-all-start.1 = ((s32[16,1,128]{2,1,0:T(1,128)}), s32[16,1,128]{2,1,0:T(1,128)S(1)}, u32[]{:S(2)}, u32[]{:S(2)}) async-start(s32[16,1,128]{2,1,0:T(1,128)} %reshape.102), calls=%async_computation.1 | async-start | bytes 16384 | tf_op jit(solution)/shard_map/all_to_all | solution.py:94
  21.7 0.7 copy-start.5
  21.7 0.7 copy-start.4
  28.8 11.8 %all-to-all-start = ((f32[16,16,5]{1,2,0:T(8,128)}), f32[16,16,5]{1,2,0:T(8,128)S(1)}, u32[]{:S(2)}, u32[]{:S(2)}) async-start(f32[16,16,5]{1,2,0:T(8,128)} %stack.3), calls=%async_computation | async-start | bytes 131072 | tf_op jit(solution)/shard_map/all_to_all | solution.py:93
  32.7 7.8 %copy-start = (f32[8,3,8,3]{2,3,1,0:T(4,128)S(1)}, f32[8,3,8,3]{2,3,1,0:T(4,128)}, u32[]{:S(2)}) copy-start(f32[8,3,8,3]{2,3,1,0:T(4,128)} %constant.33.clone..sunk.3) | copy-start | bytes 6916
  32.7 7.8 %copy-start.2 = (f32[8,3,8,3]{2,3,1,0:T(4,128)S(1)}, f32[8,3,8,3]{2,3,1,0:T(4,128)}, u32[]{:S(2)}) copy-start(f32[8,3,8,3]{2,3,1,0:T(4,128)} %constant.51) | copy-start | bytes 6916
where the time goes:
time: 123 us
  blocking collectives  40.7 us (33%)
  other arithmetic  22.1 us (18%)
  matrix products  21.7 us (18%)
  starting transfers between devices  13.9 us (11%)
  waiting for transfers between devices  12.2 us (10%)
  local copies, waits for them, and re-layouts  9.53 us (8%)
  loops' own time  1.78 us (1%)
    psum x4, blocking collectives, over_axes(): return functools.reduce(lax.psum, axes, shard)  40.7 us
    dot_general x16, matrix products, assemble_block(): jnp.einsum('epa,epijb->iajb', onehot, spread, precision=lax.Precision.HIG...  11 us
    dot_general x16, matrix products, assemble_block(): jnp.einsum('epiqj,eqb->epijb', matrices, onehot, precision=lax.Precision....  10.8 us
    all_to_all x1, starting transfers between devices, on_device(): lax.all_to_all(node_ids, GZ, split_axis=0, concat_axis=0, tiled=True)  9.97 us
    all_to_all x1, waiting for transfers between devices, on_device(): params = lax.all_to_all(params, GZ, split_axis=0, concat_axis=0, tiled=True)  6.61 us
    reduce_sum x1, other arithmetic, on_device(): position = jnp.sum(onehot * node_iota, axis=3)  5.7 us
    all_to_all x1, waiting for transfers between devices, on_device(): lax.all_to_all(node_ids, GZ, split_axis=0, concat_axis=0, tiled=True)  5.63 us
    reduce_sum x1, other arithmetic, on_device(): present = jnp.sum(onehot, axis=3) > 0  4.38 us
  transfers between devices with their start and end apart: 2, of which 2 were waited for; matrix products, arithmetic and copies ran while one was open for 2% of the time, Pallas kernels for 0%

commit v1 on v0

v1 whole, which is shorter than its diff:
```python
import functools

import jax
import jax.numpy as jnp
from jax import lax
from jax.experimental import pallas as pl
from jax.experimental.pallas import tpu as pltpu
from jax.sharding import PartitionSpec as P

MESH = pl.DeviceIdType.MESH
F32, BF16 = jnp.float32, jnp.bfloat16
TILE, CAP, CORNERS = 128, 16, 8

ALL_MODES = (1, 2, 4, 3, 5, 6, 7)


def split(value):
    high = value.astype(BF16)
    return high, (value - high.astype(F32)).astype(BF16)


def swap_groups(values):
    sub = lax.broadcasted_iota(jnp.int32, (8, 128), 0)
    group = lax.broadcasted_iota(jnp.int32, (8, 128), 1) // CAP
    for bit in (1, 2, 4):
        upper_sub = (sub & bit) != 0
        upper_group = (group & bit) != 0
        below = pltpu.roll(pltpu.roll(values, 8 - bit, 0), CAP * bit, 1)
        above = pltpu.roll(pltpu.roll(values, bit, 0), 128 - CAP * bit, 1)
        values = jnp.where(
            upper_sub == upper_group, values, jnp.where(upper_sub, above, below)
        )
    return values


def kernel(
    n_x, n_y, n_z,
    live_hbm, inc_hbm, lame_hbm, shear_hbm, stretch_hbm,
    block_ref, scale_ref,
    live, inc, lame, shear, stretch, nodes, params, send, recv, plane, plane_recv, line, line_recv,
    in_sem, small_sem, send_sem, recv_sem, plane_send_sem, plane_sem, line_send_sem, line_sem,
):
    n_tiles = send.shape[0]
    my_x, my_y, my_z = lax.axis_index("gx"), lax.axis_index("gy"), lax.axis_index("gz")
    n_xy = n_x * n_y
    my_xy = my_x * n_y + my_y

    chunks = in_sem.shape[0]
    rows = inc.shape[0] // chunks
    loads = [
        pltpu.make_async_copy(
            inc_hbm.at[pl.ds(c * rows, rows)], inc.at[pl.ds(c * rows, rows)], in_sem.at[c]
        )
        for c in range(chunks)
    ]
    small = [
        pltpu.make_async_copy(source, target, small_sem.at[k])
        for k, (source, target) in enumerate(
            ((live_hbm, live), (lame_hbm, lame), (shear_hbm, shear), (stretch_hbm, stretch))
        )
    ]
    for copy in small + loads:
        copy.start()

    barrier = pltpu.get_barrier_semaphore()

    @pl.loop(1, n_z)
    def _(step):
        pl.semaphore_signal(
            barrier, inc=1, device_id={"gz": lax.rem(my_z + step, n_z)}, device_id_type=MESH
        )

    @pl.loop(1, n_xy)
    def _(step):
        other = lax.rem(my_xy + step, n_xy)
        pl.semaphore_signal(
            barrier,
            inc=1,
            device_id={"gx": other // n_y, "gy": lax.rem(other, n_y)},
            device_id_type=MESH,
        )

    for copy in small:
        copy.wait()
    params[...] = jnp.zeros_like(params)
    first, second = lame[...], shear[...]
    lengths = [stretch[k] for k in range(3)]
    for k, value in enumerate([first, second] + lengths):
        params[:, k * CAP : (k + 1) * CAP] = value
    send[:, 1, :] = params[...]
    inverse = [1.0 / value for value in lengths]
    trace = (
        (lengths[0] * lengths[1] * lengths[2] / 9.0)
        * (first + 4.0 * second)
        * (inverse[0] * inverse[0] + inverse[1] * inverse[1] + inverse[2] * inverse[2])
    )
    trace = jnp.concatenate([trace] * CORNERS, axis=1)

    number = (lax.broadcasted_iota(jnp.int32, (TILE, TILE), 0) + 1).astype(F32).astype(BF16)
    row = lax.broadcasted_iota(jnp.int32, (TILE, TILE), 0)
    lane = lax.broadcasted_iota(jnp.int32, (TILE, TILE), 1)
    place = lane == (row % CORNERS) * CAP + row // CORNERS
    slot = lax.broadcasted_iota(jnp.int32, (1, TILE), 1) % CAP
    per_chunk = n_tiles // chunks
    for t in range(n_tiles):
        if t % per_chunk == 0:
            loads[t // per_chunk].wait()
        onehot = inc[t * TILE : (t + 1) * TILE, :].astype(F32).astype(BF16)
        spread = jnp.dot(onehot, number, preferred_element_type=F32)
        ids = jnp.sum(jnp.where(place, spread, 0.0), axis=0, keepdims=True)
        ids = jnp.where(slot < live[0, t], ids, 0.0)
        send[t, 0:1, :] = ids
        nodes[t : t + 1, :] = ids
    partial = jnp.sum(jnp.where(nodes[...] > 0.0, trace, 0.0), axis=0, keepdims=True)
    plane[...] = jnp.broadcast_to(jnp.sum(partial, axis=1, keepdims=True), (1, TILE))

    pl.semaphore_wait(barrier, (n_z - 1) + (n_xy - 1))

    def to_plane(step):
        other = lax.rem(my_xy + step, n_xy)
        return pltpu.make_async_remote_copy(
            src_ref=plane,
            dst_ref=plane_recv.at[my_xy],
            send_sem=plane_send_sem.at[step],
            recv_sem=plane_sem.at[my_xy],
            device_id={"gx": other // n_y, "gy": lax.rem(other, n_y)},
            device_id_type=MESH,
        )

    def to_tile(step):
        other = lax.rem(my_z + step, n_z)
        return pltpu.make_async_remote_copy(
            src_ref=send.at[other],
            dst_ref=recv.at[my_z],
            send_sem=send_sem.at[step],
            recv_sem=recv_sem.at[my_z],
            device_id={"gz": other},
            device_id_type=MESH,
        )

    def to_line(step):
        other = lax.rem(my_z + step, n_z)
        return pltpu.make_async_remote_copy(
            src_ref=line,
            dst_ref=line_recv.at[my_z],
            send_sem=line_send_sem.at[step],
            recv_sem=line_sem.at[my_z],
            device_id={"gz": other},
            device_id_type=MESH,
        )

    def await_from(target, sems, source, device):
        pltpu.make_async_remote_copy(
            src_ref=target.at[source],
            dst_ref=target.at[source],
            send_sem=sems.at[source],
            recv_sem=sems.at[source],
            device_id=device,
            device_id_type=MESH,
        ).wait_recv()

    @pl.loop(1, n_xy)
    def _(step):
        to_plane(step).start()

    @pl.loop(1, n_z)
    def _(step):
        to_tile(step).start()

    recv[my_z] = send[my_z]
    plane_recv[my_xy] = plane[...]

    @pl.loop(1, n_xy)
    def _(step):
        other = lax.rem(my_xy + step, n_xy)
        await_from(plane_recv, plane_sem, other, {"gx": other // n_y, "gy": lax.rem(other, n_y)})

    total = plane_recv[0]
    for k in range(1, n_xy):
        total = total + plane_recv[k]
    line[...] = total
    line_recv[my_z] = total

    @pl.loop(1, n_z)
    def _(step):
        to_line(step).start()

    @pl.loop(1, n_z)
    def _(step):
        other = lax.rem(my_z + step, n_z)
        await_from(recv, recv_sem, other, {"gz": other})

    halves = range(n_z // 8)
    ids = jnp.concatenate([swap_groups(recv[8 * h : 8 * h + 8, 0, :]) for h in halves], axis=1)
    material = jnp.concatenate(
        [swap_groups(recv[8 * h : 8 * h + 8, 1, :]) for h in halves], axis=1
    )
    wide = ids.shape[1]
    first, second = material[0:1], material[1:2]
    h = [material[2 + k : 3 + k] for k in range(3)]

    node = (lax.broadcasted_iota(jnp.int32, (TILE, wide), 0) + 1).astype(F32)
    corner = [
        jnp.where(node == ids[p : p + 1], 1.0, 0.0).astype(BF16) for p in range(CORNERS)
    ]
    mode = corner
    for bit in (1, 2, 4):
        mode = [
            mode[k] - mode[k ^ bit] if k & bit else mode[k] + mode[k ^ bit]
            for k in range(CORNERS)
        ]

    def scaled(wave, coefficient):
        wide_row = jnp.broadcast_to(coefficient, (16, wide)).astype(BF16)
        return (wave.reshape(TILE // 16, 16, wide) * wide_row[None]).reshape(TILE, wide)

    def product(left, right):
        return lax.dot_general(
            left, right, (((1,), (1,)), ((), ())), preferred_element_type=F32
        )

    def assemble(pairs):
        high, low, other = [], [], []
        for left, right, coefficient in pairs:
            top = coefficient.astype(BF16).astype(F32)
            high.append(scaled(mode[left], top))
            low.append(scaled(mode[left], coefficient - top))
            other.append(mode[right])
        right = jnp.concatenate(other, axis=1)
        left = jnp.concatenate(
            [jnp.concatenate(high, axis=1), jnp.concatenate(low, axis=1)], axis=0
        )
        result = product(left, right)
        return result[:TILE] + result[TILE:]

    area = [h[1] * h[2] / (16.0 * h[0]), h[0] * h[2] / (16.0 * h[1]), h[0] * h[1] / (16.0 * h[2])]
    strong = first + 2.0 * second
    for i in range(3):
        alpha = [(strong if k == i else second) * area[k] for k in range(3)]
        coefficients = {
            1: alpha[0],
            2: alpha[1],
            4: alpha[2],
            3: (alpha[0] + alpha[1]) / 3.0,
            5: (alpha[0] + alpha[2]) / 3.0,
            6: (alpha[1] + alpha[2]) / 3.0,
            7: (alpha[0] + alpha[1] + alpha[2]) / 9.0,
        }
        block_ref[i, i] = assemble([(m, m, coefficients[m]) for m in ALL_MODES])
    for i, j, k in ((0, 1, 2), (0, 2, 1), (1, 2, 0)):
        a, b, c = 1 << i, 1 << j, 1 << k
        la, mu = h[k] * first / 16.0, h[k] * second / 16.0
        result = assemble(
            [
                (a, b, la),
                (a | c, b | c, la / 3.0),
                (b, a, mu),
                (b | c, a | c, mu / 3.0),
            ]
        )
        block_ref[i, j] = result
        block_ref[j, i] = result.T

    @pl.loop(1, n_z)
    def _(step):
        other = lax.rem(my_z + step, n_z)
        await_from(line_recv, line_sem, other, {"gz": other})

    total = line_recv[0]
    for k in range(1, n_z):
        total = total + line_recv[k]
    scale_ref[...] = (3.0 * TILE * n_xy * n_z) / total

    @pl.loop(1, n_xy)
    def _(step):
        to_plane(step).wait_send()

    @pl.loop(1, n_z)
    def _(step):
        to_tile(step).wait_send()
        to_line(step).wait_send()


def solution(mesh):
    n_x, n_y, n_z = mesh.shape["gx"], mesh.shape["gy"], mesh.shape["gz"]
    n_xy = n_x * n_y

    def on_device(incidence, live_counts, lame_first, shear_modulus, stretch):
        n_tiles = incidence.shape[3]
        hbm = pl.BlockSpec(memory_space=pl.ANY)
        vmem = pl.BlockSpec(memory_space=pltpu.VMEM)
        block, scale = pl.pallas_call(
            functools.partial(kernel, n_x, n_y, n_z),
            out_shape=(
                jax.ShapeDtypeStruct((3, 3, TILE, TILE), F32),
                jax.ShapeDtypeStruct((1, TILE), F32),
            ),
            in_specs=[hbm] * 5,
            out_specs=(vmem, vmem),
            scratch_shapes=[
                pltpu.SMEM((1, n_tiles), jnp.int32),
                pltpu.VMEM((n_tiles * CAP * CORNERS, TILE), jnp.int32),
                pltpu.VMEM((n_tiles, CAP), F32),
                pltpu.VMEM((n_tiles, CAP), F32),
                pltpu.VMEM((3, n_tiles, CAP), F32),
                pltpu.VMEM((n_tiles, TILE), F32),
                pltpu.VMEM((n_tiles, TILE), F32),
                pltpu.VMEM((n_z, 2, TILE), F32),
                pltpu.VMEM((n_z, 2, TILE), F32),
                pltpu.VMEM((1, TILE), F32),
                pltpu.VMEM((n_xy, 1, TILE), F32),
                pltpu.VMEM((1, TILE), F32),
                pltpu.VMEM((n_z, 1, TILE), F32),
                pltpu.SemaphoreType.DMA((4,)),
                pltpu.SemaphoreType.DMA((4,)),
                pltpu.SemaphoreType.DMA((n_z,)),
                pltpu.SemaphoreType.DMA((n_z,)),
                pltpu.SemaphoreType.DMA((n_xy,)),
                pltpu.SemaphoreType.DMA((n_xy,)),
                pltpu.SemaphoreType.DMA((n_z,)),
                pltpu.SemaphoreType.DMA((n_z,)),
            ],
            compiler_params=pltpu.CompilerParams(collective_id=0, has_side_effects=True),
        )(
            live_counts.reshape(1, n_tiles),
            incidence.reshape(n_tiles * CAP * CORNERS, TILE),
            lame_first.reshape(n_tiles, CAP),
            shear_modulus.reshape(n_tiles, CAP),
            stretch.reshape(3, n_tiles, CAP),
        )
        block = block * scale.reshape(1, 1, 1, TILE)
        return block.transpose(0, 2, 1, 3).reshape(1, 1, 1, 3, TILE, 3, TILE)

    return jax.shard_map(
        on_device,
        mesh=mesh,
        in_specs=(
            P("gx", "gy", "gz", None, None, None, None),
            P("gx", "gy", "gz", None),
            P("gx", "gy", "gz", None, None),
            P("gx", "gy", "gz", None, None),
            P(None, "gx", "gy", "gz", None, None),
        ),
        out_specs=P("gx", "gy", "gz", None, None, None, None),
        check_vma=False,
    )
```

time: 123 us -> 24 us (0.20)
  blocking collectives: 40.7 us -> 0 us
  matrix products: 21.7 us -> 0 us
  Pallas kernels: 0 us -> 21.3 us
  other arithmetic: 22.1 us -> 1.93 us
  starting transfers between devices: 13.9 us -> 0 us
  waiting for transfers between devices: 12.2 us -> 0 us
  local copies, waits for them, and re-layouts: 9.53 us -> 0.66 us
  loops' own time: 1.78 us -> 0 us
    psum x4 -> x0, blocking collectives: 40.7 us -> none  [over_axes(): return functools.reduce(lax.psum, axes, shard)]
    dot_general x32 -> x0, matrix products: 21.7 us -> none  [the longest x16 11 us: assemble_block(): jnp.einsum('epa,epijb->iajb', onehot, spread, precision=lax.Precision.HIG...]
    pallas_call x0 -> x1, Pallas kernels: none -> 21.3 us  [on_device(): pl.pallas_call(functools.partial(kernel, n_x, n_y, n_z), out_shape=(jax.S...]
    all_to_all x2 -> x0, starting transfers between devices: 13.9 us -> none  [the longest x1 9.97 us: on_device(): lax.all_to_all(node_ids, GZ, split_axis=0, concat_axis=0, tiled=True)]
    all_to_all x2 -> x0, waiting for transfers between devices: 12.2 us -> none  [the longest x1 6.61 us: on_device(): params = lax.all_to_all(params, GZ, split_axis=0, concat_axis=0, tiled=True)]
    reduce_sum x3 -> x0, other arithmetic: 10.9 us -> none  [the longest x1 5.7 us: on_device(): position = jnp.sum(onehot * node_iota, axis=3)]
    mul x64 -> x0, other arithmetic: 6.14 us -> none  [the longest x16 3.72 us: element_matrices(): return matrices * volume[:, None, None, None, None]]
    mul x32 -> x0, local copies, waits for them, and re-layouts: 4.45 us -> none  [the longest x16 4.37 us: element_matrices(): return matrices * volume[:, None, None, None, None]]
  transfers between devices with their start and end apart: 2 -> 0, of which waited for: 2 -> 0; matrix products, arithmetic and copies ran while one was open for 2% -> 0% of each run, Pallas kernels for 0% -> 0%
where the time goes in v1:
time: 24 us; the launch traced here: 23.9 us
  Pallas kernels  21.3 us (89%)
  other arithmetic  1.93 us (8%)
  local copies, waits for them, and re-layouts  0.66 us (3%)
    pallas_call x1, Pallas kernels, on_device(): pl.pallas_call(functools.partial(kernel, n_x, n_y, n_z), out_shape=(jax.S...  21.3 us
    reshape x1, other arithmetic, on_device(): return block.transpose(0, 2, 1, 3).reshape(1, 1, 1, 3, TILE, 3, TILE)  1.93 us
    unnamed x2, local copies, waits for them, and re-layouts  0.66 us

profile of v1, /device:TPU:1, one launch (start us, length us, event | category | flops | bytes accessed | tf_op | source)
XLA Modules:
  0.0 23.9 jit_solution(1078508510059969805)
XLA Ops:
  0.0 21.3 %shard_map.55 = (f32[3,3,128,128]{3,2,1,0:T(8,128)}, f32[1,128]{1,0:T(1,128)}) custom-call(s32[1,16]{1,0:T(1,128)} %bitcast.14, s32[2048,128]{1,0:T(8,128)} %bitcast.10, f32[16,16]{1,0:T(8,128)} %bitcast.12, f32[16,16]{1,0:T(8,128)} %bitcast.13, f32[3,16,16]{2,1,0:T(8,128)} %bitcast.11), custom_call_target="tpu_custom_call" | custom-call | tf_op jit(solution)/shard_map/pallas_call | solution.py:292
  21.3 0.0 copy-start
  21.3 0.7 %copy-done = f32[1,128]{1,0:T(1,128)S(1)} copy-done((f32[1,128]{1,0:T(1,128)S(1)}, f32[1,128]{1,0:T(1,128)}, u32[]{:S(2)}) %copy-start) | copy-done | bytes 536
  21.9 1.9 %multiply_bitcast_fusion = f32[1,1,1,3,128,3,128]{6,4,5,3,2,1,0:T(8,128)} fusion(f32[3,3,128,128]{3,2,1,0:T(8,128)} %get-tuple-element.7, f32[128]{0:T(128)S(1)} %bitcast.15), kind=kLoop, calls=%fused_computation | loop fusion | flops 147456 | bytes 1180160 | tf_op jit(solution)/shard_map/reshape | solution.py:332
Async XLA Ops:
  21.3 0.7 %copy-start = (f32[1,128]{1,0:T(1,128)S(1)}, f32[1,128]{1,0:T(1,128)}, u32[]{:S(2)}) copy-start(f32[1,128]{1,0:T(1,128)} %get-tuple-element.8) | copy-start | bytes 1540

commit v2 on v1

--- a/solution.py
+++ b/solution.py
@@ -37,13 +37,12 @@
     n_x, n_y, n_z,
     live_hbm, inc_hbm, lame_hbm, shear_hbm, stretch_hbm,
     block_ref, scale_ref,
-    live, inc, lame, shear, stretch, nodes, params, send, recv, plane, plane_recv, line, line_recv,
-    in_sem, small_sem, send_sem, recv_sem, plane_send_sem, plane_sem, line_send_sem, line_sem,
+    live, inc, lame, shear, stretch, nodes, params, send, recv, plane_recv, line_recv,
+    in_sem, small_sem, send_sem, recv_sem,
 ):
     n_tiles = send.shape[0]
     my_x, my_y, my_z = lax.axis_index("gx"), lax.axis_index("gy"), lax.axis_index("gz")
     n_xy = n_x * n_y
-    my_xy = my_x * n_y + my_y
 
     chunks = in_sem.shape[0]
     rows = inc.shape[0] // chunks
@@ -62,23 +61,26 @@
     for copy in small + loads:
         copy.start()
 
+    at_x = [lax.rem(my_x + k, n_x) for k in range(n_x)]
+    at_y = [lax.rem(my_y + k, n_y) for k in range(n_y)]
+    at_z = [lax.rem(my_z + k, n_z) for k in range(n_z)]
+
+    def hops(step, size):
+        return min(step, size - step)
+
+    plane_steps = sorted(
+        ((i, j) for i in range(n_x) for j in range(n_y) if i or j),
+        key=lambda step: -hops(step[0], n_x) - hops(step[1], n_y),
+    )
+    line_steps = sorted(range(1, n_z), key=lambda step: -hops(step, n_z))
+
     barrier = pltpu.get_barrier_semaphore()
-
-    @pl.loop(1, n_z)
-    def _(step):
+    for i, j in plane_steps:
         pl.semaphore_signal(
-            barrier, inc=1, device_id={"gz": lax.rem(my_z + step, n_z)}, device_id_type=MESH
-        )
-
-    @pl.loop(1, n_xy)
-    def _(step):
-        other = lax.rem(my_xy + step, n_xy)
-        pl.semaphore_signal(
-            barrier,
-            inc=1,
-            device_id={"gx": other // n_y, "gy": lax.rem(other, n_y)},
-            device_id_type=MESH,
-        )
+            barrier, inc=1, device_id={"gx": at_x[i], "gy": at_y[j]}, device_id_type=MESH
+        )
+    for step in line_steps:
+        pl.semaphore_signal(barrier, inc=1, device_id={"gz": at_z[step]}, device_id_type=MESH)
 
     for copy in small:
         copy.wait()
@@ -112,83 +114,59 @@
         send[t, 0:1, :] = ids
         nodes[t : t + 1, :] = ids
     partial = jnp.sum(jnp.where(nodes[...] > 0.0, trace, 0.0), axis=0, keepdims=True)
-    plane[...] = jnp.broadcast_to(jnp.sum(partial, axis=1, keepdims=True), (1, TILE))
+    plane_recv[0] = jnp.broadcast_to(jnp.sum(partial, axis=1, keepdims=True), (1, TILE))
 
     pl.semaphore_wait(barrier, (n_z - 1) + (n_xy - 1))
 
-    def to_plane(step):
-        other = lax.rem(my_xy + step, n_xy)
+    for i, j in plane_steps:
+        pltpu.make_async_remote_copy(
+            src_ref=plane_recv.at[0],
+            dst_ref=plane_recv.at[i * n_y + j],
+            send_sem=send_sem.at[0],
+            recv_sem=recv_sem.at[0],
+            device_id={"gx": at_x[i], "gy": at_y[j]},
+            device_id_type=MESH,
+        ).start()
+    for step in line_steps:
+        pltpu.make_async_remote_copy(
+            src_ref=send.at[at_z[step]],
+            dst_ref=recv.at[step],
+            send_sem=send_sem.at[1],
+            recv_sem=recv_sem.at[1],
+            device_id={"gz": at_z[step]},
+            device_id_type=MESH,
+        ).start()
+    recv[0] = send[my_z]
+
+    def whole(target, kind, device):
         return pltpu.make_async_remote_copy(
-            src_ref=plane,
-            dst_ref=plane_recv.at[my_xy],
-            send_sem=plane_send_sem.at[step],
-            recv_sem=plane_sem.at[my_xy],
-            device_id={"gx": other // n_y, "gy": lax.rem(other, n_y)},
-            device_id_type=MESH,
-        )
-
-    def to_tile(step):
-        other = lax.rem(my_z + step, n_z)
-        return pltpu.make_async_remote_copy(
-            src_ref=send.at[other],
-            dst_ref=recv.at[my_z],
-            send_sem=send_sem.at[step],
-            recv_sem=recv_sem.at[my_z],
-            device_id={"gz": other},
-            device_id_type=MESH,
-        )
-
-    def to_line(step):
-        other = lax.rem(my_z + step, n_z)
-        return pltpu.make_async_remote_copy(
-            src_ref=line,
-            dst_ref=line_recv.at[my_z],
-            send_sem=line_send_sem.at[step],
-            recv_sem=line_sem.at[my_z],
-            device_id={"gz": other},
-            device_id_type=MESH,
-        )
-
-    def await_from(target, sems, source, device):
-        pltpu.make_async_remote_copy(
-            src_ref=target.at[source],
-            dst_ref=target.at[source],
-            send_sem=sems.at[source],
-            recv_sem=sems.at[source],
+            src_ref=target.at[pl.ds(1, target.shape[0] - 1)],
+            dst_ref=target.at[pl.ds(1, target.shape[0] - 1)],
+            send_sem=send_sem.at[kind],
+            recv_sem=recv_sem.at[kind],
             device_id=device,
             device_id_type=MESH,
-        ).wait_recv()
-
-    @pl.loop(1, n_xy)
-    def _(step):
-        to_plane(step).start()
-
-    @pl.loop(1, n_z)
-    def _(step):
-        to_tile(step).start()
-
-    recv[my_z] = send[my_z]
-    plane_recv[my_xy] = plane[...]
-
-    @pl.loop(1, n_xy)
-    def _(step):
-        other = lax.rem(my_xy + step, n_xy)
-        await_from(plane_recv, plane_sem, other, {"gx": other // n_y, "gy": lax.rem(other, n_y)})
-
+        )
+
+    plane_all = whole(plane_recv, 0, {"gx": at_x[n_x - 1], "gy": at_y[n_y - 1]})
+    tile_all = whole(recv, 1, {"gz": at_z[1]})
+    line_all = whole(line_recv, 2, {"gz": at_z[1]})
+
+    plane_all.wait_recv()
     total = plane_recv[0]
     for k in range(1, n_xy):
         total = total + plane_recv[k]
-    line[...] = total
-    line_recv[my_z] = total
-
-    @pl.loop(1, n_z)
-    def _(step):
-        to_line(step).start()
-
-    @pl.loop(1, n_z)
-    def _(step):
-        other = lax.rem(my_z + step, n_z)
-        await_from(recv, recv_sem, other, {"gz": other})
+    line_recv[0] = total
+    for step in line_steps:
+        pltpu.make_async_remote_copy(
+            src_ref=line_recv.at[0],
+            dst_ref=line_recv.at[step],
+            send_sem=send_sem.at[2],
+            recv_sem=recv_sem.at[2],
+            device_id={"gz": at_z[step]},
+            device_id_type=MESH,
+        ).start()
+    tile_all.wait_recv()
 
     halves = range(n_z // 8)
     ids = jnp.concatenate([swap_groups(recv[8 * h : 8 * h + 8, 0, :]) for h in halves], axis=1)
@@ -261,24 +239,13 @@
         block_ref[i, j] = result
         block_ref[j, i] = result.T
 
-    @pl.loop(1, n_z)
-    def _(step):
-        other = lax.rem(my_z + step, n_z)
-        await_from(line_recv, line_sem, other, {"gz": other})
-
+    line_all.wait_recv()
     total = line_recv[0]
     for k in range(1, n_z):
         total = total + line_recv[k]
     scale_ref[...] = (3.0 * TILE * n_xy * n_z) / total
-
-    @pl.loop(1, n_xy)
-    def _(step):
-        to_plane(step).wait_send()
-
-    @pl.loop(1, n_z)
-    def _(step):
-        to_tile(step).wait_send()
-        to_line(step).wait_send()
+    for copies in (plane_all, tile_all, line_all):
+        copies.wait_send()
 
 
 def solution(mesh):
@@ -287,7 +254,7 @@
 
     def on_device(incidence, live_counts, lame_first, shear_modulus, stretch):
         n_tiles = incidence.shape[3]
-        hbm = pl.BlockSpec(memory_space=pl.ANY)
+        hbm = pl.BlockSpec(memory_space=pltpu.HBM)
         vmem = pl.BlockSpec(memory_space=pltpu.VMEM)
         block, scale = pl.pallas_call(
             functools.partial(kernel, n_x, n_y, n_z),
@@ -307,26 +274,27 @@
                 pltpu.VMEM((n_tiles, TILE), F32),
                 pltpu.VMEM((n_z, 2, TILE), F32),
                 pltpu.VMEM((n_z, 2, TILE), F32),
-                pltpu.VMEM((1, TILE), F32),
                 pltpu.VMEM((n_xy, 1, TILE), F32),
-                pltpu.VMEM((1, TILE), F32),
                 pltpu.VMEM((n_z, 1, TILE), F32),
+                pltpu.SemaphoreType.DMA((8,)),
                 pltpu.SemaphoreType.DMA((4,)),
-                pltpu.SemaphoreType.DMA((4,)),
-                pltpu.SemaphoreType.DMA((n_z,)),
-                pltpu.SemaphoreType.DMA((n_z,)),
-                pltpu.SemaphoreType.DMA((n_xy,)),
-                pltpu.SemaphoreType.DMA((n_xy,)),
-                pltpu.SemaphoreType.DMA((n_z,)),
-                pltpu.SemaphoreType.DMA((n_z,)),
+                pltpu.SemaphoreType.DMA((3,)),
+                pltpu.SemaphoreType.DMA((3,)),
             ],
-            compiler_params=pltpu.CompilerParams(collective_id=0, has_side_effects=True),
+            compiler_params=pltpu.CompilerParams(
+                collective_id=0, has_side_effects=True, vmem_limit_bytes=24 << 20
+            ),
         )(
-            live_counts.reshape(1, n_tiles),
-            incidence.reshape(n_tiles * CAP * CORNERS, TILE),
-            lame_first.reshape(n_tiles, CAP),
-            shear_modulus.reshape(n_tiles, CAP),
-            stretch.reshape(3, n_tiles, CAP),
+            *(
+                pltpu.with_memory_space_constraint(value, pltpu.HBM)
+                for value in (
+                    live_counts.reshape(1, n_tiles),
+                    incidence.reshape(n_tiles * CAP * CORNERS, TILE),
+                    lame_first.reshape(n_tiles, CAP),
+                    shear_modulus.reshape(n_tiles, CAP),
+                    stretch.reshape(3, n_tiles, CAP),
+                )
+            )
         )
         block = block * scale.reshape(1, 1, 1, TILE)
         return block.transpose(0, 2, 1, 3).reshape(1, 1, 1, 3, TILE, 3, TILE)

time: 24 us -> 20.5 us (0.85)
  Pallas kernels: 21.3 us -> 19.5 us
  other arithmetic: 1.93 us -> 0.86 us
  local copies, waits for them, and re-layouts: 0.66 us -> 0 us
    pallas_call x1, Pallas kernels: 21.3 us -> 19.5 us  [on_device(): pl.pallas_call(functools.partial(kernel, n_x, n_y, n_z), out_shape=(jax.S...]
    reshape x1, other arithmetic: 1.93 us -> 0.86 us  [on_device(): return block.transpose(0, 2, 1, 3).reshape(1, 1, 1, 3, TILE, 3, TILE)]
    unnamed x2 -> x0, local copies, waits for them, and re-layouts: 0.66 us -> none
where the time goes in v2:
time: 20.5 us; the launch traced here: 20.4 us
  Pallas kernels  19.5 us (95%)
  other arithmetic  0.86 us (4%)
    pallas_call x1, Pallas kernels, on_device(): pl.pallas_call(functools.partial(kernel, n_x, n_y, n_z), out_shape=(jax.S...  19.5 us
    reshape x1, other arithmetic, on_device(): return block.transpose(0, 2, 1, 3).reshape(1, 1, 1, 3, TILE, 3, TILE)  0.86 us

profile of v2, /device:TPU:1, one launch (start us, length us, event | category | flops | bytes accessed | tf_op | source)
XLA Modules:
  0.0 20.4 jit_solution(13542598971037575050)
XLA Ops:
  0.0 19.5 %shard_map.55 = (f32[3,3,128,128]{3,2,1,0:T(8,128)S(1)}, f32[1,128]{1,0:T(1,128)S(1)}) custom-call(s32[1,16]{1,0:T(1,128)} %bitcast.15, s32[2048,128]{1,0:T(8,128)} %bitcast.11, f32[16,16]{1,0:T(8,128)} %bitcast.13, f32[16,16]{1,0:T(8,128)} %bitcast.14, f32[3,16,16]{2,1,0:T(8,128)} %bitcast.12), custom_call_target="tpu_custom_call" | custom-call | tf_op jit(solution)/shard_map/pallas_call | solution.py:259
  19.6 0.9 %multiply_bitcast_fusion = f32[1,1,1,3,128,3,128]{6,4,5,3,2,1,0:T(8,128)} fusion(f32[3,3,128,128]{3,2,1,0:T(8,128)S(1)} %get-tuple-element.7, f32[128]{0:T(128)S(1)} %bitcast.10), kind=kLoop, calls=%fused_computation | loop fusion | flops 147456 | bytes 1180160 | tf_op jit(solution)/shard_map/reshape | solution.py:300

commit v3 on v2

--- a/solution.py
+++ b/solution.py
@@ -10,6 +10,8 @@
 MESH = pl.DeviceIdType.MESH
 F32, BF16 = jnp.float32, jnp.bfloat16
 TILE, CAP, CORNERS = 128, 16, 8
+
+HUB = (0, 0, 1)
 
 ALL_MODES = (1, 2, 4, 3, 5, 6, 7)
 
@@ -38,6 +40,7 @@
     live_hbm, inc_hbm, lame_hbm, shear_hbm, stretch_hbm,
     block_ref, scale_ref,
     live, inc, lame, shear, stretch, nodes, params, send, recv, plane_recv, line_recv,
+    hub_recv,
     in_sem, small_sem, send_sem, recv_sem,
 ):
     n_tiles = send.shape[0]
@@ -81,6 +84,30 @@
         )
     for step in line_steps:
         pl.semaphore_signal(barrier, inc=1, device_id={"gz": at_z[step]}, device_id_type=MESH)
+
+    hub_x, hub_y, hub_z = HUB
+    hub_line = jnp.logical_and(my_x == hub_x, my_y == hub_y)
+    is_hub = jnp.logical_and(hub_line, my_z == hub_z)
+
+    @pl.when(is_hub)
+    def _():
+        @pl.loop(0, n_xy)
+        def _(step):
+            far = lax.rem(step + n_xy // 2 + n_y // 2, n_xy)
+            target = {"gx": lax.rem(hub_x + far // n_y, n_x), "gy": lax.rem(hub_y + far, n_y)}
+            for k in line_steps:
+                pl.semaphore_signal(
+                    barrier,
+                    inc=1,
+                    device_id=target | {"gz": (hub_z + k) % n_z},
+                    device_id_type=MESH,
+                )
+
+            @pl.when(far > 0)
+            def _():
+                pl.semaphore_signal(
+                    barrier, inc=1, device_id=target | {"gz": hub_z}, device_id_type=MESH
+                )
 
     for copy in small:
         copy.wait()
@@ -116,7 +143,27 @@
     partial = jnp.sum(jnp.where(nodes[...] > 0.0, trace, 0.0), axis=0, keepdims=True)
     plane_recv[0] = jnp.broadcast_to(jnp.sum(partial, axis=1, keepdims=True), (1, TILE))
 
-    pl.semaphore_wait(barrier, (n_z - 1) + (n_xy - 1))
+    pl.semaphore_wait(barrier, jnp.where(is_hub, n_z + n_xy - 2, n_z + n_xy - 1))
+
+    hub_slot = (
+        lax.rem(my_x - hub_x + n_x, n_x) * n_y + lax.rem(my_y - hub_y + n_y, n_y)
+    ) * n_z + lax.rem(my_z - hub_z + n_z, n_z)
+    to_hub = pltpu.make_async_remote_copy(
+        src_ref=plane_recv.at[0],
+        dst_ref=hub_recv.at[hub_slot],
+        send_sem=send_sem.at[3],
+        recv_sem=recv_sem.at[3],
+        device_id={"gx": hub_x, "gy": hub_y, "gz": hub_z},
+        device_id_type=MESH,
+    )
+
+    @pl.when(jnp.logical_not(is_hub))
+    def _():
+        to_hub.start()
+
+    @pl.when(is_hub)
+    def _():
+        hub_recv[0] = plane_recv[0]
 
     for i, j in plane_steps:
         pltpu.make_async_remote_copy(
@@ -138,10 +185,10 @@
         ).start()
     recv[0] = send[my_z]
 
-    def whole(target, kind, device):
+    def whole(target, kind, device, fewer=0):
         return pltpu.make_async_remote_copy(
-            src_ref=target.at[pl.ds(1, target.shape[0] - 1)],
-            dst_ref=target.at[pl.ds(1, target.shape[0] - 1)],
+            src_ref=target.at[pl.ds(1, target.shape[0] - 1 - fewer)],
+            dst_ref=target.at[pl.ds(1, target.shape[0] - 1 - fewer)],
             send_sem=send_sem.at[kind],
             recv_sem=recv_sem.at[kind],
             device_id=device,
@@ -151,6 +198,8 @@
     plane_all = whole(plane_recv, 0, {"gx": at_x[n_x - 1], "gy": at_y[n_y - 1]})
     tile_all = whole(recv, 1, {"gz": at_z[1]})
     line_all = whole(line_recv, 2, {"gz": at_z[1]})
+    line_some = whole(line_recv, 2, {"gz": at_z[1]}, fewer=1)
+    hub_all = whole(hub_recv, 3, {"gz": at_z[1]})
 
     plane_all.wait_recv()
     total = plane_recv[0]
@@ -158,14 +207,18 @@
         total = total + plane_recv[k]
     line_recv[0] = total
     for step in line_steps:
-        pltpu.make_async_remote_copy(
-            src_ref=line_recv.at[0],
-            dst_ref=line_recv.at[step],
-            send_sem=send_sem.at[2],
-            recv_sem=recv_sem.at[2],
-            device_id={"gz": at_z[step]},
-            device_id_type=MESH,
-        ).start()
+
+        @pl.when(jnp.logical_not(jnp.logical_and(hub_line, at_z[step] == hub_z)))
+        def _():
+            pltpu.make_async_remote_copy(
+                src_ref=line_recv.at[0],
+                dst_ref=line_recv.at[step],
+                send_sem=send_sem.at[2],
+                recv_sem=recv_sem.at[2],
+                device_id={"gz": at_z[step]},
+                device_id_type=MESH,
+            ).start()
+
     tile_all.wait_recv()
 
     halves = range(n_z // 8)
@@ -239,13 +292,39 @@
         block_ref[i, j] = result
         block_ref[j, i] = result.T
 
-    line_all.wait_recv()
-    total = line_recv[0]
-    for k in range(1, n_z):
-        total = total + line_recv[k]
-    scale_ref[...] = (3.0 * TILE * n_xy * n_z) / total
-    for copies in (plane_all, tile_all, line_all):
-        copies.wait_send()
+    def sum_rows(rows, count):
+        lanes = min(8, count)
+        sums = [rows[k] for k in range(lanes)]
+        for k in range(lanes, count):
+            sums[k % lanes] = sums[k % lanes] + rows[k]
+        while len(sums) > 1:
+            sums = [sums[k] + sums[k + 1] for k in range(0, len(sums), 2)]
+        return sums[0]
+
+    entries = 3.0 * TILE * n_xy * n_z
+
+    @pl.when(is_hub)
+    def _():
+        hub_all.wait_recv()
+        scale_ref[...] = entries / sum_rows(hub_recv, n_xy * n_z)
+
+    @pl.when(jnp.logical_not(is_hub))
+    def _():
+        line_all.wait_recv()
+        scale_ref[...] = entries / sum_rows(line_recv, n_z)
+        to_hub.wait_send()
+
+    plane_all.wait_send()
+    tile_all.wait_send()
+    in_between = jnp.logical_and(hub_line, my_z != hub_z)
+
+    @pl.when(in_between)
+    def _():
+        line_some.wait_send()
+
+    @pl.when(jnp.logical_not(in_between))
+    def _():
+        line_all.wait_send()
 
 
 def solution(mesh):
@@ -276,10 +355,11 @@
                 pltpu.VMEM((n_z, 2, TILE), F32),
                 pltpu.VMEM((n_xy, 1, TILE), F32),
                 pltpu.VMEM((n_z, 1, TILE), F32),
-                pltpu.SemaphoreType.DMA((8,)),
+                pltpu.VMEM((n_xy * n_z, 1, TILE), F32),
                 pltpu.SemaphoreType.DMA((4,)),
-                pltpu.SemaphoreType.DMA((3,)),
-                pltpu.SemaphoreType.DMA((3,)),
+                pltpu.SemaphoreType.DMA((4,)),
+                pltpu.SemaphoreType.DMA((4,)),
+                pltpu.SemaphoreType.DMA((4,)),
             ],
             compiler_params=pltpu.CompilerParams(
                 collective_id=0, has_side_effects=True, vmem_limit_bytes=24 << 20

time: 20.5 us -> 18.3 us (0.89)
  Pallas kernels: 19.5 us -> 17.4 us
    pallas_call x1, Pallas kernels: 19.5 us -> 17.4 us  [on_device(): pl.pallas_call(functools.partial(kernel, n_x, n_y, n_z), out_shape=(jax.S...]
where the time goes in v3:
time: 18.3 us; the launch traced here: 18.2 us
  Pallas kernels  17.4 us (95%)
  other arithmetic  0.86 us (5%)
    pallas_call x1, Pallas kernels, on_device(): pl.pallas_call(functools.partial(kernel, n_x, n_y, n_z), out_shape=(jax.S...  17.4 us
    reshape x1, other arithmetic, on_device(): return block.transpose(0, 2, 1, 3).reshape(1, 1, 1, 3, TILE, 3, TILE)  0.86 us

profile of v3, /device:TPU:1, one launch (start us, length us, event | category | flops | bytes accessed | tf_op | source)
XLA Modules:
  0.0 18.2 jit_solution(3392972077968421618)
XLA Ops:
  0.0 17.4 %shard_map.55 = (f32[3,3,128,128]{3,2,1,0:T(8,128)S(1)}, f32[1,128]{1,0:T(1,128)S(1)}) custom-call(s32[1,16]{1,0:T(1,128)} %bitcast.15, s32[2048,128]{1,0:T(8,128)} %bitcast.11, f32[16,16]{1,0:T(8,128)} %bitcast.13, f32[16,16]{1,0:T(8,128)} %bitcast.14, f32[3,16,16]{2,1,0:T(8,128)} %bitcast.12), custom_call_target="tpu_custom_call" | custom-call | tf_op jit(solution)/shard_map/pallas_call | solution.py:338
  17.4 0.9 %multiply_bitcast_fusion = f32[1,1,1,3,128,3,128]{6,4,5,3,2,1,0:T(8,128)} fusion(f32[3,3,128,128]{3,2,1,0:T(8,128)S(1)} %get-tuple-element.7, f32[128]{0:T(128)S(1)} %bitcast.10), kind=kLoop, calls=%fused_computation | loop fusion | flops 147456 | bytes 1180160 | tf_op jit(solution)/shard_map/reshape | solution.py:380

commit v4 on v2

--- a/solution.py
+++ b/solution.py
@@ -10,6 +10,10 @@
 MESH = pl.DeviceIdType.MESH
 F32, BF16 = jnp.float32, jnp.bfloat16
 TILE, CAP, CORNERS = 128, 16, 8
+
+LEAD = 1
+CAST = 3
+EARLY = 4
 
 ALL_MODES = (1, 2, 4, 3, 5, 6, 7)
 
@@ -37,8 +41,8 @@
     n_x, n_y, n_z,
     live_hbm, inc_hbm, lame_hbm, shear_hbm, stretch_hbm,
     block_ref, scale_ref,
-    live, inc, lame, shear, stretch, nodes, params, send, recv, plane_recv, line_recv,
-    in_sem, small_sem, send_sem, recv_sem,
+    live, inc, lame, shear, stretch, nodes, params, send, recv, row, row_recv, hub_recv,
+    in_sem, small_sem, send_sem, recv_sem, cast_sem, here, ready,
 ):
     n_tiles = send.shape[0]
     my_x, my_y, my_z = lax.axis_index("gx"), lax.axis_index("gy"), lax.axis_index("gz")
@@ -58,29 +62,59 @@
             ((live_hbm, live), (lame_hbm, lame), (shear_hbm, shear), (stretch_hbm, stretch))
         )
     ]
-    for copy in small + loads:
+    for copy in loads + small:
         copy.start()
-
-    at_x = [lax.rem(my_x + k, n_x) for k in range(n_x)]
-    at_y = [lax.rem(my_y + k, n_y) for k in range(n_y)]
-    at_z = [lax.rem(my_z + k, n_z) for k in range(n_z)]
 
     def hops(step, size):
         return min(step, size - step)
 
+    hubs = [(0, 0, LEAD), (0, 0, CAST)]
+    hubs += [(i, 0, LEAD) for i in range(1, n_x)] + [(0, j, LEAD) for j in range(1, n_y)]
+
+    def is_at(x, y, z):
+        return jnp.logical_and(jnp.logical_and(my_x == x, my_y == y), my_z == z)
+
+    in_corner = jnp.logical_and(my_x == 0, my_y == 0)
+    on_edge = jnp.logical_or(my_x == 0, my_y == 0)
+    is_lead = my_z == LEAD
+    is_early = my_z < EARLY
+    is_hub = jnp.logical_or(jnp.logical_and(on_edge, is_lead), is_at(0, 0, CAST))
     plane_steps = sorted(
-        ((i, j) for i in range(n_x) for j in range(n_y) if i or j),
+        ((i, j) for i in range(n_x) for j in range(n_y)),
         key=lambda step: -hops(step[0], n_x) - hops(step[1], n_y),
     )
     line_steps = sorted(range(1, n_z), key=lambda step: -hops(step, n_z))
 
     barrier = pltpu.get_barrier_semaphore()
-    for i, j in plane_steps:
+
+    def greet(x, y, z):
         pl.semaphore_signal(
-            barrier, inc=1, device_id={"gx": at_x[i], "gy": at_y[j]}, device_id_type=MESH
-        )
-    for step in line_steps:
-        pl.semaphore_signal(barrier, inc=1, device_id={"gz": at_z[step]}, device_id_type=MESH)
+            barrier, inc=1, device_id={"gx": x, "gy": y, "gz": z}, device_id_type=MESH
+        )
+
+    @pl.when(is_early)
+    def _():
+        for step in line_steps:
+            greet(my_x, my_y, lax.rem(my_z + step, n_z))
+
+    @pl.when(is_hub)
+    def _():
+        half = n_z // 2
+
+        @pl.loop(0, half)
+        def _(near):
+            ahead = lax.rem(my_z + half + near, n_z)
+            behind = lax.rem(my_z + jnp.where(near == 0, 0, half - near), n_z)
+            for i, j in plane_steps:
+                x, y = lax.rem(my_x + i, n_x), lax.rem(my_y + j, n_y)
+                greet(x, y, ahead)
+                if i or j:
+                    greet(x, y, behind)
+                else:
+
+                    @pl.when(near > 0)
+                    def _():
+                        greet(x, y, behind)
 
     for copy in small:
         copy.wait()
@@ -99,9 +133,9 @@
     trace = jnp.concatenate([trace] * CORNERS, axis=1)
 
     number = (lax.broadcasted_iota(jnp.int32, (TILE, TILE), 0) + 1).astype(F32).astype(BF16)
-    row = lax.broadcasted_iota(jnp.int32, (TILE, TILE), 0)
+    down = lax.broadcasted_iota(jnp.int32, (TILE, TILE), 0)
     lane = lax.broadcasted_iota(jnp.int32, (TILE, TILE), 1)
-    place = lane == (row % CORNERS) * CAP + row // CORNERS
+    place = lane == (down % CORNERS) * CAP + down // CORNERS
     slot = lax.broadcasted_iota(jnp.int32, (1, TILE), 1) % CAP
     per_chunk = n_tiles // chunks
     for t in range(n_tiles):
@@ -114,59 +148,76 @@
         send[t, 0:1, :] = ids
         nodes[t : t + 1, :] = ids
     partial = jnp.sum(jnp.where(nodes[...] > 0.0, trace, 0.0), axis=0, keepdims=True)
-    plane_recv[0] = jnp.broadcast_to(jnp.sum(partial, axis=1, keepdims=True), (1, TILE))
-
-    pl.semaphore_wait(barrier, (n_z - 1) + (n_xy - 1))
-
-    for i, j in plane_steps:
-        pltpu.make_async_remote_copy(
-            src_ref=plane_recv.at[0],
-            dst_ref=plane_recv.at[i * n_y + j],
-            send_sem=send_sem.at[0],
-            recv_sem=recv_sem.at[0],
-            device_id={"gx": at_x[i], "gy": at_y[j]},
+    row[...] = jnp.broadcast_to(jnp.sum(partial, axis=1, keepdims=True), (1, TILE))
+
+    pl.semaphore_wait(
+        barrier,
+        len(hubs) + EARLY - jnp.where(is_hub, 1, 0) - jnp.where(is_early, 1, 0),
+    )
+
+    for x, y, z in hubs:
+        source = lax.rem(my_x - x + n_x, n_x) * n_y + lax.rem(my_y - y + n_y, n_y)
+
+        @pl.when(jnp.logical_not(is_at(x, y, z)))
+        def _():
+            pltpu.make_async_remote_copy(
+                src_ref=row,
+                dst_ref=hub_recv.at[source * n_z + lax.rem(my_z - z + n_z, n_z)],
+                send_sem=send_sem.at[0],
+                recv_sem=recv_sem.at[0],
+                device_id={"gx": x, "gy": y, "gz": z},
+                device_id_type=MESH,
+            ).start()
+
+    hub_recv[0] = row[...]
+
+    @pl.when(jnp.logical_not(is_lead))
+    def _():
+        pl.semaphore_signal(here, inc=1, device_id={"gz": LEAD}, device_id_type=MESH)
+
+    def send_tile(z):
+        @pl.when(my_z != z)
+        def _():
+            pltpu.make_async_remote_copy(
+                src_ref=send.at[z],
+                dst_ref=recv.at[lax.rem(my_z - z + n_z, n_z)],
+                send_sem=send_sem.at[1],
+                recv_sem=recv_sem.at[1],
+                device_id={"gz": z},
+                device_id_type=MESH,
+            ).start()
+
+    for z in range(EARLY):
+        send_tile(z)
+    recv[0] = send[my_z]
+
+    @pl.when(is_lead)
+    def _():
+        pl.semaphore_wait(here, n_z - 1)
+        for step in line_steps:
+            pl.semaphore_signal(
+                ready, inc=1, device_id={"gz": (LEAD + step) % n_z}, device_id_type=MESH
+            )
+
+    @pl.when(jnp.logical_not(is_lead))
+    def _():
+        pl.semaphore_wait(ready, 1)
+
+    for z in range(EARLY, n_z):
+        send_tile(z)
+
+    def rows(target, count, send_with, recv_with):
+        return pltpu.make_async_remote_copy(
+            src_ref=target.at[pl.ds(1, count)],
+            dst_ref=target.at[pl.ds(1, count)],
+            send_sem=send_with,
+            recv_sem=recv_with,
+            device_id={"gz": lax.rem(my_z + 1, n_z)},
             device_id_type=MESH,
-        ).start()
-    for step in line_steps:
-        pltpu.make_async_remote_copy(
-            src_ref=send.at[at_z[step]],
-            dst_ref=recv.at[step],
-            send_sem=send_sem.at[1],
-            recv_sem=recv_sem.at[1],
-            device_id={"gz": at_z[step]},
-            device_id_type=MESH,
-        ).start()
-    recv[0] = send[my_z]
-
-    def whole(target, kind, device):
-        return pltpu.make_async_remote_copy(
-            src_ref=target.at[pl.ds(1, target.shape[0] - 1)],
-            dst_ref=target.at[pl.ds(1, target.shape[0] - 1)],
-            send_sem=send_sem.at[kind],
-            recv_sem=recv_sem.at[kind],
-            device_id=device,
-            device_id_type=MESH,
-        )
-
-    plane_all = whole(plane_recv, 0, {"gx": at_x[n_x - 1], "gy": at_y[n_y - 1]})
-    tile_all = whole(recv, 1, {"gz": at_z[1]})
-    line_all = whole(line_recv, 2, {"gz": at_z[1]})
-
-    plane_all.wait_recv()
-    total = plane_recv[0]
-    for k in range(1, n_xy):
-        total = total + plane_recv[k]
-    line_recv[0] = total
-    for step in line_steps:
-        pltpu.make_async_remote_copy(
-            src_ref=line_recv.at[0],
-            dst_ref=line_recv.at[step],
-            send_sem=send_sem.at[2],
-            recv_sem=recv_sem.at[2],
-            device_id={"gz": at_z[step]},
-            device_id_type=MESH,
-        ).start()
-    tile_all.wait_recv()
+        )
+
+    tiles = rows(recv, n_z - 1, send_sem.at[1], recv_sem.at[1])
+    tiles.wait_recv()
 
     halves = range(n_z // 8)
     ids = jnp.concatenate([swap_groups(recv[8 * h : 8 * h + 8, 0, :]) for h in halves], axis=1)
@@ -239,13 +290,80 @@
         block_ref[i, j] = result
         block_ref[j, i] = result.T
 
-    line_all.wait_recv()
-    total = line_recv[0]
-    for k in range(1, n_z):
-        total = total + line_recv[k]
-    scale_ref[...] = (3.0 * TILE * n_xy * n_z) / total
-    for copies in (plane_all, tile_all, line_all):
-        copies.wait_send()
+    def sum_rows(values, count):
+        lanes = min(8, count)
+        sums = [values[k] for k in range(lanes)]
+        for k in range(lanes, count):
+            sums[k % lanes] = sums[k % lanes] + values[k]
+        while len(sums) > 1:
+            sums = [sums[k] + sums[k + 1] for k in range(0, len(sums), 2)]
+        return sums[0]
+
+    from_x, from_y = jnp.minimum(my_x, n_x - my_x), jnp.minimum(my_y, n_y - my_y)
+    lead_x = jnp.logical_and(is_lead, jnp.logical_and(my_y == 0, my_x != 0))
+    lead_y = jnp.logical_and(is_lead, jnp.logical_and(my_x == 0, my_y != 0))
+    lines = [(0, 0, jnp.logical_and(is_hub, jnp.logical_not(is_at(0, 0, LEAD))))]
+    lines += [
+        (0, j, jnp.logical_and(lead_x, hops(j, n_y) <= from_x)) for j in range(1, n_y)
+    ]
+    lines += [(i, 0, jnp.logical_and(lead_y, from_y > hops(i, n_x))) for i in range(1, n_x)]
+
+    @pl.when(is_hub)
+    def _():
+        rows(hub_recv, n_xy * n_z - 1, send_sem.at[0], recv_sem.at[0]).wait_recv()
+        scale = (3.0 * TILE * n_xy * n_z) / sum_rows(hub_recv, n_xy * n_z)
+        scale_ref[...] = scale
+        row_recv[...] = scale
+        for which, (i, j, casts) in enumerate(lines):
+
+            @pl.when(casts)
+            def _():
+                for z in range(n_z):
+                    copy = pltpu.make_async_remote_copy(
+                        src_ref=row_recv,
+                        dst_ref=row_recv,
+                        send_sem=cast_sem.at[which],
+                        recv_sem=recv_sem.at[2],
+                        device_id={
+                            "gx": lax.rem(my_x + i, n_x),
+                            "gy": lax.rem(my_y + j, n_y),
+                            "gz": z,
+                        },
+                        device_id_type=MESH,
+                    )
+                    if i or j:
+                        copy.start()
+                    else:
+                        first_hub = jnp.logical_and(in_corner, z == LEAD)
+
+                        @pl.when(jnp.logical_not(jnp.logical_or(my_z == z, first_hub)))
+                        def _():
+                            copy.start()
+
+        for which, (i, j, casts) in enumerate(lines):
+            if i or j:
+
+                @pl.when(casts)
+                def _():
+                    rows(hub_recv, n_z, cast_sem.at[which], recv_sem.at[2]).wait_send()
+
+        @pl.when(jnp.logical_and(is_lead, jnp.logical_not(in_corner)))
+        def _():
+            rows(hub_recv, n_z - 1, cast_sem.at[0], recv_sem.at[2]).wait_send()
+
+        @pl.when(jnp.logical_not(is_lead))
+        def _():
+            rows(hub_recv, n_z - 2, cast_sem.at[0], recv_sem.at[2]).wait_send()
+
+        rows(hub_recv, len(hubs) - 1, send_sem.at[0], recv_sem.at[0]).wait_send()
+
+    @pl.when(jnp.logical_not(is_hub))
+    def _():
+        rows(hub_recv, 1, send_sem.at[2], recv_sem.at[2]).wait_recv()
+        scale_ref[...] = row_recv[...]
+        rows(hub_recv, len(hubs), send_sem.at[0], recv_sem.at[0]).wait_send()
+
+    tiles.wait_send()
 
 
 def solution(mesh):
@@ -274,12 +392,16 @@
                 pltpu.VMEM((n_tiles, TILE), F32),
                 pltpu.VMEM((n_z, 2, TILE), F32),
                 pltpu.VMEM((n_z, 2, TILE), F32),
-                pltpu.VMEM((n_xy, 1, TILE), F32),
-                pltpu.VMEM((n_z, 1, TILE), F32),
-                pltpu.SemaphoreType.DMA((8,)),
+                pltpu.VMEM((1, TILE), F32),
+                pltpu.VMEM((1, TILE), F32),
+                pltpu.VMEM((n_xy * n_z, 1, TILE), F32),
+                pltpu.SemaphoreType.DMA((4,)),
                 pltpu.SemaphoreType.DMA((4,)),
                 pltpu.SemaphoreType.DMA((3,)),
                 pltpu.SemaphoreType.DMA((3,)),
+                pltpu.SemaphoreType.DMA((n_x + n_y - 1,)),
+                pltpu.SemaphoreType.REGULAR,
+                pltpu.SemaphoreType.REGULAR,
             ],
             compiler_params=pltpu.CompilerParams(
                 collective_id=0, has_side_effects=True, vmem_limit_bytes=24 << 20

time: 20.5 us -> 17.9 us (0.87)
  Pallas kernels: 19.5 us -> 16.9 us
    pallas_call x1, Pallas kernels: 19.5 us -> 16.9 us  [on_device(): pl.pallas_call(functools.partial(kernel, n_x, n_y, n_z), out_shape=(jax.S...]
where the time goes in v4:
time: 17.9 us; the launch traced here: 17.8 us
  Pallas kernels  16.9 us (94%)
  other arithmetic  0.86 us (5%)
    pallas_call x1, Pallas kernels, on_device(): pl.pallas_call(functools.partial(kernel, n_x, n_y, n_z), out_shape=(jax.S...  16.9 us
    reshape x1, other arithmetic, on_device(): return block.transpose(0, 2, 1, 3).reshape(1, 1, 1, 3, TILE, 3, TILE)  0.86 us

profile of v4, /device:TPU:1, one launch (start us, length us, event | category | flops | bytes accessed | tf_op | source)
XLA Modules:
  0.0 17.8 jit_solution(3295219092649893690)
XLA Ops:
  0.0 16.9 %shard_map.55 = (f32[3,3,128,128]{3,2,1,0:T(8,128)S(1)}, f32[1,128]{1,0:T(1,128)S(1)}) custom-call(s32[1,16]{1,0:T(1,128)} %bitcast.15, s32[2048,128]{1,0:T(8,128)} %bitcast.11, f32[16,16]{1,0:T(8,128)} %bitcast.13, f32[16,16]{1,0:T(8,128)} %bitcast.14, f32[3,16,16]{2,1,0:T(8,128)} %bitcast.12), custom_call_target="tpu_custom_call" | custom-call | tf_op jit(solution)/shard_map/pallas_call | solution.py:377
  16.9 0.9 %multiply_bitcast_fusion = f32[1,1,1,3,128,3,128]{6,4,5,3,2,1,0:T(8,128)} fusion(f32[3,3,128,128]{3,2,1,0:T(8,128)S(1)} %get-tuple-element.7, f32[128]{0:T(128)S(1)} %bitcast.10), kind=kLoop, calls=%fused_computation | loop fusion | flops 147456 | bytes 1180160 | tf_op jit(solution)/shard_map/reshape | solution.py:422

commit v5 on v4

--- a/solution.py
+++ b/solution.py
@@ -41,28 +41,21 @@
     n_x, n_y, n_z,
     live_hbm, inc_hbm, lame_hbm, shear_hbm, stretch_hbm,
     block_ref, scale_ref,
-    live, inc, lame, shear, stretch, nodes, params, send, recv, row, row_recv, hub_recv,
+    live, inc, lame, shear, stretch, weight, number, place, params, send, recv, row, row_recv, hub_recv,
     in_sem, small_sem, send_sem, recv_sem, cast_sem, here, ready,
 ):
     n_tiles = send.shape[0]
     my_x, my_y, my_z = lax.axis_index("gx"), lax.axis_index("gy"), lax.axis_index("gz")
     n_xy = n_x * n_y
 
-    chunks = in_sem.shape[0]
-    rows = inc.shape[0] // chunks
-    loads = [
-        pltpu.make_async_copy(
-            inc_hbm.at[pl.ds(c * rows, rows)], inc.at[pl.ds(c * rows, rows)], in_sem.at[c]
-        )
-        for c in range(chunks)
-    ]
+    load = pltpu.make_async_copy(inc_hbm, inc, in_sem)
     small = [
         pltpu.make_async_copy(source, target, small_sem.at[k])
         for k, (source, target) in enumerate(
             ((live_hbm, live), (lame_hbm, lame), (shear_hbm, shear), (stretch_hbm, stretch))
         )
     ]
-    for copy in loads + small:
+    for copy in [load] + small:
         copy.start()
 
     def hops(step, size):
@@ -130,24 +123,29 @@
         * (first + 4.0 * second)
         * (inverse[0] * inverse[0] + inverse[1] * inverse[1] + inverse[2] * inverse[2])
     )
-    trace = jnp.concatenate([trace] * CORNERS, axis=1)
-
-    number = (lax.broadcasted_iota(jnp.int32, (TILE, TILE), 0) + 1).astype(F32).astype(BF16)
+    diagonal = lax.broadcasted_iota(jnp.int32, (CAP, CAP), 0) == lax.broadcasted_iota(
+        jnp.int32, (CAP, CAP), 1
+    )
+    slot_down = lax.broadcasted_iota(jnp.int32, (CAP, 1), 0)
+    for t in range(n_tiles):
+        column = jnp.sum(jnp.where(diagonal, trace[t : t + 1, :], 0.0), axis=1, keepdims=True)
+        column = jnp.where(slot_down < live[0, t], column, 0.0)
+        weight[t * CAP : (t + 1) * CAP, :] = jnp.broadcast_to(column, (CAP, TILE))
+
     down = lax.broadcasted_iota(jnp.int32, (TILE, TILE), 0)
     lane = lax.broadcasted_iota(jnp.int32, (TILE, TILE), 1)
-    place = lane == (down % CORNERS) * CAP + down // CORNERS
+    number[...] = (down + 1).astype(F32).astype(BF16)
+    place[...] = jnp.where(lane == (down % CORNERS) * CAP + down // CORNERS, 1.0, 0.0)
     slot = lax.broadcasted_iota(jnp.int32, (1, TILE), 1) % CAP
-    per_chunk = n_tiles // chunks
-    for t in range(n_tiles):
-        if t % per_chunk == 0:
-            loads[t // per_chunk].wait()
-        onehot = inc[t * TILE : (t + 1) * TILE, :].astype(F32).astype(BF16)
-        spread = jnp.dot(onehot, number, preferred_element_type=F32)
-        ids = jnp.sum(jnp.where(place, spread, 0.0), axis=0, keepdims=True)
-        ids = jnp.where(slot < live[0, t], ids, 0.0)
-        send[t, 0:1, :] = ids
-        nodes[t : t + 1, :] = ids
-    partial = jnp.sum(jnp.where(nodes[...] > 0.0, trace, 0.0), axis=0, keepdims=True)
+
+    load.wait()
+    sums = [jnp.zeros((CORNERS, TILE), F32) for _ in range(8)]
+    for e in range(n_tiles * CAP):
+        onehot = inc[e * CORNERS : (e + 1) * CORNERS, :].astype(F32)
+        sums[e % 8] = sums[e % 8] + onehot * weight[e : e + 1, :]
+    while len(sums) > 1:
+        sums = [sums[k] + sums[k + 1] for k in range(0, len(sums), 2)]
+    partial = jnp.sum(sums[0], axis=0, keepdims=True)
     row[...] = jnp.broadcast_to(jnp.sum(partial, axis=1, keepdims=True), (1, TILE))
 
     pl.semaphore_wait(
@@ -174,6 +172,12 @@
     @pl.when(jnp.logical_not(is_lead))
     def _():
         pl.semaphore_signal(here, inc=1, device_id={"gz": LEAD}, device_id_type=MESH)
+
+    for t in range(n_tiles):
+        onehot = inc[t * TILE : (t + 1) * TILE, :].astype(F32).astype(BF16)
+        spread = jnp.dot(onehot, number[...], preferred_element_type=F32)
+        ids = jnp.sum(spread * place[...], axis=0, keepdims=True)
+        send[t, 0:1, :] = jnp.where(slot < live[0, t], ids, 0.0)
 
     def send_tile(z):
         @pl.when(my_z != z)
@@ -388,14 +392,16 @@
                 pltpu.VMEM((n_tiles, CAP), F32),
                 pltpu.VMEM((n_tiles, CAP), F32),
                 pltpu.VMEM((3, n_tiles, CAP), F32),
-                pltpu.VMEM((n_tiles, TILE), F32),
+                pltpu.VMEM((n_tiles * CAP, TILE), F32),
+                pltpu.VMEM((TILE, TILE), BF16),
+                pltpu.VMEM((TILE, TILE), F32),
                 pltpu.VMEM((n_tiles, TILE), F32),
                 pltpu.VMEM((n_z, 2, TILE), F32),
                 pltpu.VMEM((n_z, 2, TILE), F32),
                 pltpu.VMEM((1, TILE), F32),
                 pltpu.VMEM((1, TILE), F32),
                 pltpu.VMEM((n_xy * n_z, 1, TILE), F32),
-                pltpu.SemaphoreType.DMA((4,)),
+                pltpu.SemaphoreType.DMA,
                 pltpu.SemaphoreType.DMA((4,)),
                 pltpu.SemaphoreType.DMA((3,)),
                 pltpu.SemaphoreType.DMA((3,)),

time: 17.9 us -> 17.3 us (0.966)
  Pallas kernels: 16.9 us -> 16.3 us
    pallas_call x1, Pallas kernels: 16.9 us -> 16.3 us  [on_device(): pl.pallas_call(functools.partial(kernel, n_x, n_y, n_z), out_shape=(jax.S...]
where the time goes in v5:
time: 17.3 us; the launch traced here: 17.2 us
  Pallas kernels  16.3 us (94%)
  other arithmetic  0.86 us (5%)
    pallas_call x1, Pallas kernels, on_device(): pl.pallas_call(functools.partial(kernel, n_x, n_y, n_z), out_shape=(jax.S...  16.3 us
    reshape x1, other arithmetic, on_device(): return block.transpose(0, 2, 1, 3).reshape(1, 1, 1, 3, TILE, 3, TILE)  0.86 us

profile of v5, /device:TPU:1, one launch (start us, length us, event | category | flops | bytes accessed | tf_op | source)
XLA Modules:
  0.0 17.2 jit_solution(11203274404912498865)
XLA Ops:
  0.0 16.3 %shard_map.55 = (f32[3,3,128,128]{3,2,1,0:T(8,128)S(1)}, f32[1,128]{1,0:T(1,128)S(1)}) custom-call(s32[1,16]{1,0:T(1,128)} %bitcast.15, s32[2048,128]{1,0:T(8,128)} %bitcast.11, f32[16,16]{1,0:T(8,128)} %bitcast.13, f32[16,16]{1,0:T(8,128)} %bitcast.14, f32[3,16,16]{2,1,0:T(8,128)} %bitcast.12), custom_call_target="tpu_custom_call" | custom-call | tf_op jit(solution)/shard_map/pallas_call | solution.py:381
  16.4 0.9 %multiply_bitcast_fusion = f32[1,1,1,3,128,3,128]{6,4,5,3,2,1,0:T(8,128)} fusion(f32[3,3,128,128]{3,2,1,0:T(8,128)S(1)} %get-tuple-element.7, f32[128]{0:T(128)S(1)} %bitcast.10), kind=kLoop, calls=%fused_computation | loop fusion | flops 147456 | bytes 1180160 | tf_op jit(solution)/shard_map/reshape | solution.py:428

commit v6 on v5

--- a/solution.py
+++ b/solution.py
@@ -48,6 +48,16 @@
     my_x, my_y, my_z = lax.axis_index("gx"), lax.axis_index("gy"), lax.axis_index("gz")
     n_xy = n_x * n_y
 
+    last = 4
+    short = 2 * CORNERS
+    ends = [(inc.shape[0] - last * short) * k // last for k in range(last + 1)]
+    ends += [inc.shape[0] - short * k for k in range(last - 1, -1, -1)]
+    loads = [
+        pltpu.make_async_copy(
+            inc_hbm.at[pl.ds(first, end - first)], inc.at[pl.ds(first, end - first)], in_sem
+        )
+        for first, end in zip(ends, ends[1:])
+    ]
     load = pltpu.make_async_copy(inc_hbm, inc, in_sem)
     small = [
         pltpu.make_async_copy(source, target, small_sem.at[k])
@@ -55,7 +65,7 @@
             ((live_hbm, live), (lame_hbm, lame), (shear_hbm, shear), (stretch_hbm, stretch))
         )
     ]
-    for copy in [load] + small:
+    for copy in small + loads:
         copy.start()
 
     def hops(step, size):
@@ -318,46 +328,48 @@
         scale = (3.0 * TILE * n_xy * n_z) / sum_rows(hub_recv, n_xy * n_z)
         scale_ref[...] = scale
         row_recv[...] = scale
-        for which, (i, j, casts) in enumerate(lines):
-
-            @pl.when(casts)
-            def _():
-                for z in range(n_z):
-                    copy = pltpu.make_async_remote_copy(
-                        src_ref=row_recv,
-                        dst_ref=row_recv,
-                        send_sem=cast_sem.at[which],
-                        recv_sem=recv_sem.at[2],
-                        device_id={
-                            "gx": lax.rem(my_x + i, n_x),
-                            "gy": lax.rem(my_y + j, n_y),
-                            "gz": z,
-                        },
-                        device_id_type=MESH,
-                    )
-                    if i or j:
-                        copy.start()
-                    else:
-                        first_hub = jnp.logical_and(in_corner, z == LEAD)
-
-                        @pl.when(jnp.logical_not(jnp.logical_or(my_z == z, first_hub)))
-                        def _():
-                            copy.start()
-
-        for which, (i, j, casts) in enumerate(lines):
-            if i or j:
+        @pl.when(jnp.logical_not(is_at(0, 0, LEAD)))
+        def _():
+            for which, (i, j, casts) in enumerate(lines):
 
                 @pl.when(casts)
                 def _():
-                    rows(hub_recv, n_z, cast_sem.at[which], recv_sem.at[2]).wait_send()
-
-        @pl.when(jnp.logical_and(is_lead, jnp.logical_not(in_corner)))
-        def _():
-            rows(hub_recv, n_z - 1, cast_sem.at[0], recv_sem.at[2]).wait_send()
-
-        @pl.when(jnp.logical_not(is_lead))
-        def _():
-            rows(hub_recv, n_z - 2, cast_sem.at[0], recv_sem.at[2]).wait_send()
+                    for z in range(n_z):
+                        copy = pltpu.make_async_remote_copy(
+                            src_ref=row_recv,
+                            dst_ref=row_recv,
+                            send_sem=cast_sem.at[which],
+                            recv_sem=recv_sem.at[2],
+                            device_id={
+                                "gx": lax.rem(my_x + i, n_x),
+                                "gy": lax.rem(my_y + j, n_y),
+                                "gz": z,
+                            },
+                            device_id_type=MESH,
+                        )
+                        if i or j:
+                            copy.start()
+                        else:
+                            first_hub = jnp.logical_and(in_corner, z == LEAD)
+
+                            @pl.when(jnp.logical_not(jnp.logical_or(my_z == z, first_hub)))
+                            def _():
+                                copy.start()
+
+            for which, (i, j, casts) in enumerate(lines):
+                if i or j:
+
+                    @pl.when(casts)
+                    def _():
+                        rows(hub_recv, n_z, cast_sem.at[which], recv_sem.at[2]).wait_send()
+
+            @pl.when(jnp.logical_and(is_lead, jnp.logical_not(in_corner)))
+            def _():
+                rows(hub_recv, n_z - 1, cast_sem.at[0], recv_sem.at[2]).wait_send()
+
+            @pl.when(jnp.logical_not(is_lead))
+            def _():
+                rows(hub_recv, n_z - 2, cast_sem.at[0], recv_sem.at[2]).wait_send()
 
         rows(hub_recv, len(hubs) - 1, send_sem.at[0], recv_sem.at[0]).wait_send()
 

time: 17.3 us -> 17.4 us (level)
  no operation moved by 1% of the time
where the time goes in v6:
time: 17.4 us; the launch traced here: 17.3 us
  Pallas kernels  16.4 us (94%)
  other arithmetic  0.86 us (5%)
    pallas_call x1, Pallas kernels, on_device(): pl.pallas_call(functools.partial(kernel, n_x, n_y, n_z), out_shape=(jax.S...  16.4 us
    reshape x1, other arithmetic, on_device(): return block.transpose(0, 2, 1, 3).reshape(1, 1, 1, 3, TILE, 3, TILE)  0.86 us

profile of v6, /device:TPU:1, one launch (start us, length us, event | category | flops | bytes accessed | tf_op | source)
XLA Modules:
  0.0 17.3 jit_solution(136205457403601381)
XLA Ops:
  0.0 16.4 %shard_map.55 = (f32[3,3,128,128]{3,2,1,0:T(8,128)S(1)}, f32[1,128]{1,0:T(1,128)S(1)}) custom-call(s32[1,16]{1,0:T(1,128)} %bitcast.15, s32[2048,128]{1,0:T(8,128)} %bitcast.11, f32[16,16]{1,0:T(8,128)} %bitcast.13, f32[16,16]{1,0:T(8,128)} %bitcast.14, f32[3,16,16]{2,1,0:T(8,128)} %bitcast.12), custom_call_target="tpu_custom_call" | custom-call | tf_op jit(solution)/shard_map/pallas_call | solution.py:393
  16.4 0.9 %multiply_bitcast_fusion = f32[1,1,1,3,128,3,128]{6,4,5,3,2,1,0:T(8,128)} fusion(f32[3,3,128,128]{3,2,1,0:T(8,128)S(1)} %get-tuple-element.7, f32[128]{0:T(128)S(1)} %bitcast.10), kind=kLoop, calls=%fused_computation | loop fusion | flops 147456 | bytes 1180160 | tf_op jit(solution)/shard_map/reshape | solution.py:440

commit v7 on v6

--- a/solution.py
+++ b/solution.py
@@ -50,15 +50,22 @@
 
     last = 4
     short = 2 * CORNERS
-    ends = [(inc.shape[0] - last * short) * k // last for k in range(last + 1)]
-    ends += [inc.shape[0] - short * k for k in range(last - 1, -1, -1)]
+    main = inc.shape[0] - last * short
+    ends = [main // CORNERS * k // last * CORNERS for k in range(last + 1)]
+    ends += [main + short * (k + 1) for k in range(last)]
     loads = [
         pltpu.make_async_copy(
-            inc_hbm.at[pl.ds(first, end - first)], inc.at[pl.ds(first, end - first)], in_sem
-        )
-        for first, end in zip(ends, ends[1:])
+            inc_hbm.at[pl.ds(first, end - first)],
+            inc.at[pl.ds(first, end - first)],
+            in_sem.at[min(k, last)],
+        )
+        for k, (first, end) in enumerate(zip(ends, ends[1:]))
     ]
-    load = pltpu.make_async_copy(inc_hbm, inc, in_sem)
+    rest = pl.ds(main, last * short)
+    arrivals = loads[:last] + [
+        pltpu.make_async_copy(inc_hbm.at[rest], inc.at[rest], in_sem.at[last])
+    ]
+    starts = {end // CORNERS: copy for end, copy in zip(ends, arrivals)}
     small = [
         pltpu.make_async_copy(source, target, small_sem.at[k])
         for k, (source, target) in enumerate(
@@ -148,9 +155,10 @@
     place[...] = jnp.where(lane == (down % CORNERS) * CAP + down // CORNERS, 1.0, 0.0)
     slot = lax.broadcasted_iota(jnp.int32, (1, TILE), 1) % CAP
 
-    load.wait()
     sums = [jnp.zeros((CORNERS, TILE), F32) for _ in range(8)]
     for e in range(n_tiles * CAP):
+        if e in starts:
+            starts[e].wait()
         onehot = inc[e * CORNERS : (e + 1) * CORNERS, :].astype(F32)
         sums[e % 8] = sums[e % 8] + onehot * weight[e : e + 1, :]
     while len(sums) > 1:
@@ -322,6 +330,13 @@
     ]
     lines += [(i, 0, jnp.logical_and(lead_y, from_y > hops(i, n_x))) for i in range(1, n_x)]
 
+    owned_at_x = {
+        i: 1 + sum(hops(j, n_y) <= hops(i, n_x) for j in range(1, n_y)) for i in range(1, n_x)
+    }
+    owned_at_y = {
+        j: 1 + sum(hops(j, n_y) > hops(i, n_x) for i in range(1, n_x)) for j in range(1, n_y)
+    }
+
     @pl.when(is_hub)
     def _():
         rows(hub_recv, n_xy * n_z - 1, send_sem.at[0], recv_sem.at[0]).wait_recv()
@@ -330,7 +345,7 @@
         row_recv[...] = scale
         @pl.when(jnp.logical_not(is_at(0, 0, LEAD)))
         def _():
-            for which, (i, j, casts) in enumerate(lines):
+            for i, j, casts in lines:
 
                 @pl.when(casts)
                 def _():
@@ -338,7 +353,7 @@
                         copy = pltpu.make_async_remote_copy(
                             src_ref=row_recv,
                             dst_ref=row_recv,
-                            send_sem=cast_sem.at[which],
+                            send_sem=cast_sem,
                             recv_sem=recv_sem.at[2],
                             device_id={
                                 "gx": lax.rem(my_x + i, n_x),
@@ -356,20 +371,19 @@
                             def _():
                                 copy.start()
 
-            for which, (i, j, casts) in enumerate(lines):
-                if i or j:
-
-                    @pl.when(casts)
-                    def _():
-                        rows(hub_recv, n_z, cast_sem.at[which], recv_sem.at[2]).wait_send()
-
-            @pl.when(jnp.logical_and(is_lead, jnp.logical_not(in_corner)))
-            def _():
-                rows(hub_recv, n_z - 1, cast_sem.at[0], recv_sem.at[2]).wait_send()
-
-            @pl.when(jnp.logical_not(is_lead))
-            def _():
-                rows(hub_recv, n_z - 2, cast_sem.at[0], recv_sem.at[2]).wait_send()
+            for owned in sorted({0} | set(owned_at_x.values()) | set(owned_at_y.values())):
+                own = n_z - 1 if owned else n_z - 2
+                is_so = is_at(0, 0, CAST) if owned == 0 else False
+                for i, count in owned_at_x.items():
+                    if count == owned:
+                        is_so = jnp.logical_or(is_so, is_at(i, 0, LEAD))
+                for j, count in owned_at_y.items():
+                    if count == owned:
+                        is_so = jnp.logical_or(is_so, is_at(0, j, LEAD))
+
+                @pl.when(is_so)
+                def _():
+                    rows(hub_recv, max(owned - 1, 0) * n_z + own, cast_sem, recv_sem.at[2]).wait_send()
 
         rows(hub_recv, len(hubs) - 1, send_sem.at[0], recv_sem.at[0]).wait_send()
 
@@ -413,11 +427,11 @@
                 pltpu.VMEM((1, TILE), F32),
                 pltpu.VMEM((1, TILE), F32),
                 pltpu.VMEM((n_xy * n_z, 1, TILE), F32),
-                pltpu.SemaphoreType.DMA,
+                pltpu.SemaphoreType.DMA((5,)),
                 pltpu.SemaphoreType.DMA((4,)),
                 pltpu.SemaphoreType.DMA((3,)),
                 pltpu.SemaphoreType.DMA((3,)),
-                pltpu.SemaphoreType.DMA((n_x + n_y - 1,)),
+                pltpu.SemaphoreType.DMA,
                 pltpu.SemaphoreType.REGULAR,
                 pltpu.SemaphoreType.REGULAR,
             ],

time: 17.4 us -> 17.4 us (level)
  no operation moved by 1% of the time
where the time goes in v7:
time: 17.4 us; the launch traced here: 17.3 us
  Pallas kernels  16.4 us (94%)
  other arithmetic  0.86 us (5%)
    pallas_call x1, Pallas kernels, on_device(): pl.pallas_call(functools.partial(kernel, n_x, n_y, n_z), out_shape=(jax.S...  16.4 us
    reshape x1, other arithmetic, on_device(): return block.transpose(0, 2, 1, 3).reshape(1, 1, 1, 3, TILE, 3, TILE)  0.86 us

profile of v7, /device:TPU:1, one launch (start us, length us, event | category | flops | bytes accessed | tf_op | source)
XLA Modules:
  0.0 17.3 jit_solution(17167474212814144882)
XLA Ops:
  0.0 16.4 %shard_map.55 = (f32[3,3,128,128]{3,2,1,0:T(8,128)S(1)}, f32[1,128]{1,0:T(1,128)S(1)}) custom-call(s32[1,16]{1,0:T(1,128)} %bitcast.15, s32[2048,128]{1,0:T(8,128)} %bitcast.11, f32[16,16]{1,0:T(8,128)} %bitcast.13, f32[16,16]{1,0:T(8,128)} %bitcast.14, f32[3,16,16]{2,1,0:T(8,128)} %bitcast.12), custom_call_target="tpu_custom_call" | custom-call | tf_op jit(solution)/shard_map/pallas_call | solution.py:407
  16.4 0.9 %multiply_bitcast_fusion = f32[1,1,1,3,128,3,128]{6,4,5,3,2,1,0:T(8,128)} fusion(f32[3,3,128,128]{3,2,1,0:T(8,128)S(1)} %get-tuple-element.7, f32[128]{0:T(128)S(1)} %bitcast.10), kind=kLoop, calls=%fused_computation | loop fusion | flops 147456 | bytes 1180160 | tf_op jit(solution)/shard_map/reshape | solution.py:454

commit v8 on v7

--- a/solution.py
+++ b/solution.py
@@ -41,38 +41,35 @@
     n_x, n_y, n_z,
     live_hbm, inc_hbm, lame_hbm, shear_hbm, stretch_hbm,
     block_ref, scale_ref,
-    live, inc, lame, shear, stretch, weight, number, place, params, send, recv, row, row_recv, hub_recv,
-    in_sem, small_sem, send_sem, recv_sem, cast_sem, here, ready,
+    live, inc, tail, lame, shear, stretch, alive, weight, number, place, params, send, recv, row, row_recv, hub_recv,
+    tail_sem, in_sem, send_sem, recv_sem, cast_sem, here, ready,
 ):
     n_tiles = send.shape[0]
     my_x, my_y, my_z = lax.axis_index("gx"), lax.axis_index("gy"), lax.axis_index("gz")
     n_xy = n_x * n_y
 
     last = 4
-    short = 2 * CORNERS
-    main = inc.shape[0] - last * short
-    ends = [main // CORNERS * k // last * CORNERS for k in range(last + 1)]
-    ends += [main + short * (k + 1) for k in range(last)]
+    main = inc.shape[0] - 2 * CORNERS
+    ends = [main // CORNERS * k // last * CORNERS for k in range(last + 1)] + [main + CORNERS]
+    tail_load = pltpu.make_async_copy(
+        inc_hbm.at[pl.ds(main + CORNERS, CORNERS)], tail, tail_sem
+    )
+    small = [
+        pltpu.make_async_copy(source, target, in_sem.at[k])
+        for k, (source, target) in enumerate(
+            ((live_hbm, live), (lame_hbm, lame), (shear_hbm, shear), (stretch_hbm, stretch))
+        )
+    ]
     loads = [
         pltpu.make_async_copy(
             inc_hbm.at[pl.ds(first, end - first)],
             inc.at[pl.ds(first, end - first)],
-            in_sem.at[min(k, last)],
+            in_sem.at[len(small) + k],
         )
         for k, (first, end) in enumerate(zip(ends, ends[1:]))
     ]
-    rest = pl.ds(main, last * short)
-    arrivals = loads[:last] + [
-        pltpu.make_async_copy(inc_hbm.at[rest], inc.at[rest], in_sem.at[last])
-    ]
-    starts = {end // CORNERS: copy for end, copy in zip(ends, arrivals)}
-    small = [
-        pltpu.make_async_copy(source, target, small_sem.at[k])
-        for k, (source, target) in enumerate(
-            ((live_hbm, live), (lame_hbm, lame), (shear_hbm, shear), (stretch_hbm, stretch))
-        )
-    ]
-    for copy in small + loads:
+    starts = {end // CORNERS: copy for end, copy in zip(ends, loads)}
+    for copy in [tail_load] + small + loads:
         copy.start()
 
     def hops(step, size):
@@ -143,22 +140,29 @@
     diagonal = lax.broadcasted_iota(jnp.int32, (CAP, CAP), 0) == lax.broadcasted_iota(
         jnp.int32, (CAP, CAP), 1
     )
-    slot_down = lax.broadcasted_iota(jnp.int32, (CAP, 1), 0)
+    counts = jnp.broadcast_to(live[...].astype(F32), (n_tiles, n_tiles))
+    tile_down = lax.broadcasted_iota(jnp.int32, (n_tiles, n_tiles), 0)
+    tile_across = lax.broadcasted_iota(jnp.int32, (n_tiles, n_tiles), 1)
+    counts = jnp.sum(jnp.where(tile_down == tile_across, counts, 0.0), axis=1, keepdims=True)
+    slot = lax.broadcasted_iota(jnp.int32, (n_tiles, TILE), 1) % CAP
+    alive[...] = jnp.where(slot.astype(F32) < counts, 1.0, 0.0)
+    trace = trace * alive[:, :CAP]
     for t in range(n_tiles):
         column = jnp.sum(jnp.where(diagonal, trace[t : t + 1, :], 0.0), axis=1, keepdims=True)
-        column = jnp.where(slot_down < live[0, t], column, 0.0)
         weight[t * CAP : (t + 1) * CAP, :] = jnp.broadcast_to(column, (CAP, TILE))
 
     down = lax.broadcasted_iota(jnp.int32, (TILE, TILE), 0)
     lane = lax.broadcasted_iota(jnp.int32, (TILE, TILE), 1)
     number[...] = (down + 1).astype(F32).astype(BF16)
     place[...] = jnp.where(lane == (down % CORNERS) * CAP + down // CORNERS, 1.0, 0.0)
-    slot = lax.broadcasted_iota(jnp.int32, (1, TILE), 1) % CAP
 
     sums = [jnp.zeros((CORNERS, TILE), F32) for _ in range(8)]
     for e in range(n_tiles * CAP):
         if e in starts:
             starts[e].wait()
+        if e == n_tiles * CAP - 1:
+            tail_load.wait()
+            inc[main + CORNERS : main + 2 * CORNERS, :] = tail[...]
         onehot = inc[e * CORNERS : (e + 1) * CORNERS, :].astype(F32)
         sums[e % 8] = sums[e % 8] + onehot * weight[e : e + 1, :]
     while len(sums) > 1:
@@ -195,7 +199,7 @@
         onehot = inc[t * TILE : (t + 1) * TILE, :].astype(F32).astype(BF16)
         spread = jnp.dot(onehot, number[...], preferred_element_type=F32)
         ids = jnp.sum(spread * place[...], axis=0, keepdims=True)
-        send[t, 0:1, :] = jnp.where(slot < live[0, t], ids, 0.0)
+        send[t, 0:1, :] = ids * alive[t : t + 1, :]
 
     def send_tile(z):
         @pl.when(my_z != z)
@@ -413,11 +417,13 @@
             in_specs=[hbm] * 5,
             out_specs=(vmem, vmem),
             scratch_shapes=[
-                pltpu.SMEM((1, n_tiles), jnp.int32),
+                pltpu.VMEM((1, n_tiles), jnp.int32),
                 pltpu.VMEM((n_tiles * CAP * CORNERS, TILE), jnp.int32),
+                pltpu.VMEM((CORNERS, TILE), jnp.int32),
                 pltpu.VMEM((n_tiles, CAP), F32),
                 pltpu.VMEM((n_tiles, CAP), F32),
                 pltpu.VMEM((3, n_tiles, CAP), F32),
+                pltpu.VMEM((n_tiles, TILE), F32),
                 pltpu.VMEM((n_tiles * CAP, TILE), F32),
                 pltpu.VMEM((TILE, TILE), BF16),
                 pltpu.VMEM((TILE, TILE), F32),
@@ -427,8 +433,8 @@
                 pltpu.VMEM((1, TILE), F32),
                 pltpu.VMEM((1, TILE), F32),
                 pltpu.VMEM((n_xy * n_z, 1, TILE), F32),
-                pltpu.SemaphoreType.DMA((5,)),
-                pltpu.SemaphoreType.DMA((4,)),
+                pltpu.SemaphoreType.DMA,
+                pltpu.SemaphoreType.DMA((9,)),
                 pltpu.SemaphoreType.DMA((3,)),
                 pltpu.SemaphoreType.DMA((3,)),
                 pltpu.SemaphoreType.DMA,

time: 17.4 us -> 17.2 us (0.989)
  no operation moved by 1% of the time
where the time goes in v8:
time: 17.2 us; the launch traced here: 17.1 us
  Pallas kernels  16.3 us (95%)
  other arithmetic  0.86 us (5%)
    pallas_call x1, Pallas kernels, on_device(): pl.pallas_call(functools.partial(kernel, n_x, n_y, n_z), out_shape=(jax.S...  16.3 us
    reshape x1, other arithmetic, on_device(): return block.transpose(0, 2, 1, 3).reshape(1, 1, 1, 3, TILE, 3, TILE)  0.86 us

profile of v8, /device:TPU:1, one launch (start us, length us, event | category | flops | bytes accessed | tf_op | source)
XLA Modules:
  0.0 17.1 jit_solution(10335980526171873970)
XLA Ops:
  0.0 16.3 %shard_map.55 = (f32[3,3,128,128]{3,2,1,0:T(8,128)S(1)}, f32[1,128]{1,0:T(1,128)S(1)}) custom-call(s32[1,16]{1,0:T(1,128)} %bitcast.15, s32[2048,128]{1,0:T(8,128)} %bitcast.11, f32[16,16]{1,0:T(8,128)} %bitcast.13, f32[16,16]{1,0:T(8,128)} %bitcast.14, f32[3,16,16]{2,1,0:T(8,128)} %bitcast.12), custom_call_target="tpu_custom_call" | custom-call | tf_op jit(solution)/shard_map/pallas_call | solution.py:411
  16.3 0.9 %multiply_bitcast_fusion = f32[1,1,1,3,128,3,128]{6,4,5,3,2,1,0:T(8,128)} fusion(f32[3,3,128,128]{3,2,1,0:T(8,128)S(1)} %get-tuple-element.7, f32[128]{0:T(128)S(1)} %bitcast.10), kind=kLoop, calls=%fused_computation | loop fusion | flops 147456 | bytes 1180160 | tf_op jit(solution)/shard_map/reshape | solution.py:460

commit v9 on v8

--- a/solution.py
+++ b/solution.py
@@ -182,14 +182,14 @@
         def _():
             pltpu.make_async_remote_copy(
                 src_ref=row,
-                dst_ref=hub_recv.at[source * n_z + lax.rem(my_z - z + n_z, n_z)],
+                dst_ref=hub_recv.at[my_z * n_xy + source],
                 send_sem=send_sem.at[0],
-                recv_sem=recv_sem.at[0],
+                recv_sem=recv_sem.at[jnp.where(my_z < n_z // 2, 0, 3)],
                 device_id={"gx": x, "gy": y, "gz": z},
                 device_id_type=MESH,
             ).start()
 
-    hub_recv[0] = row[...]
+    hub_recv[my_z * n_xy] = row[...]
 
     @pl.when(jnp.logical_not(is_lead))
     def _():
@@ -316,11 +316,10 @@
         block_ref[i, j] = result
         block_ref[j, i] = result.T
 
-    def sum_rows(values, count):
-        lanes = min(8, count)
-        sums = [values[k] for k in range(lanes)]
-        for k in range(lanes, count):
-            sums[k % lanes] = sums[k % lanes] + values[k]
+    def sum_rows(values, first, end):
+        sums = [values[first + k] for k in range(8)]
+        for k in range(8, end - first):
+            sums[k % 8] = sums[k % 8] + values[first + k]
         while len(sums) > 1:
             sums = [sums[k] + sums[k + 1] for k in range(0, len(sums), 2)]
         return sums[0]
@@ -343,8 +342,11 @@
 
     @pl.when(is_hub)
     def _():
-        rows(hub_recv, n_xy * n_z - 1, send_sem.at[0], recv_sem.at[0]).wait_recv()
-        scale = (3.0 * TILE * n_xy * n_z) / sum_rows(hub_recv, n_xy * n_z)
+        half = n_xy * n_z // 2
+        rows(hub_recv, half - 1, send_sem.at[0], recv_sem.at[0]).wait_recv()
+        first_half = sum_rows(hub_recv, 0, half)
+        rows(hub_recv, half, send_sem.at[0], recv_sem.at[3]).wait_recv()
+        scale = (3.0 * TILE * n_xy * n_z) / (first_half + sum_rows(hub_recv, half, 2 * half))
         scale_ref[...] = scale
         row_recv[...] = scale
         @pl.when(jnp.logical_not(is_at(0, 0, LEAD)))
@@ -398,6 +400,18 @@
         rows(hub_recv, len(hubs), send_sem.at[0], recv_sem.at[0]).wait_send()
 
     tiles.wait_send()
+
+
+def scale_kernel(block_ref, scale_ref, out_hbm, scaled, sems):
+    scale = scale_ref[...]
+    copies = []
+    for k in range(3):
+        part = pl.ds(k * 3 * TILE, 3 * TILE)
+        scaled[part, :] = block_ref[part, :] * scale
+        copies.append(pltpu.make_async_copy(scaled.at[part], out_hbm.at[part], sems.at[k]))
+        copies[k].start()
+    for copy in copies:
+        copy.wait()
 
 
 def solution(mesh):
@@ -436,7 +450,7 @@
                 pltpu.SemaphoreType.DMA,
                 pltpu.SemaphoreType.DMA((9,)),
                 pltpu.SemaphoreType.DMA((3,)),
-                pltpu.SemaphoreType.DMA((3,)),
+                pltpu.SemaphoreType.DMA((4,)),
                 pltpu.SemaphoreType.DMA,
                 pltpu.SemaphoreType.REGULAR,
                 pltpu.SemaphoreType.REGULAR,
@@ -456,7 +470,15 @@
                 )
             )
         )
-        block = block * scale.reshape(1, 1, 1, TILE)
+        block = pl.pallas_call(
+            scale_kernel,
+            out_shape=jax.ShapeDtypeStruct((9 * TILE, TILE), F32),
+            in_specs=[vmem, vmem],
+            out_specs=hbm,
+            scratch_shapes=[pltpu.VMEM((9 * TILE, TILE), F32), pltpu.SemaphoreType.DMA((3,))],
+            compiler_params=pltpu.CompilerParams(vmem_limit_bytes=24 << 20),
+        )(block.reshape(9 * TILE, TILE), scale)
+        block = block.reshape(3, 3, TILE, TILE)
         return block.transpose(0, 2, 1, 3).reshape(1, 1, 1, 3, TILE, 3, TILE)
 
     return jax.shard_map(

time: 17.2 us -> 17.2 us (level)
  other arithmetic: 0.86 us -> 0 us
  Pallas kernels: 16.3 us -> 17.1 us
    reshape x1 -> x0, other arithmetic: 0.86 us -> none  [on_device(): return block.transpose(0, 2, 1, 3).reshape(1, 1, 1, 3, TILE, 3, TILE)]
    pallas_call x0 -> x1, Pallas kernels: none -> 0.85 us  [on_device(): pl.pallas_call(scale_kernel, out_shape=jax.ShapeDtypeStruct((9 * TILE, TI...]
where the time goes in v9:
time: 17.2 us; the launch traced here: 17.1 us
  Pallas kernels  17.1 us (99%)
    pallas_call x1, Pallas kernels, on_device(): pl.pallas_call(functools.partial(kernel, n_x, n_y, n_z), out_shape=(jax.S...  16.3 us
    pallas_call x1, Pallas kernels, on_device(): pl.pallas_call(scale_kernel, out_shape=jax.ShapeDtypeStruct((9 * TILE, TI...  0.85 us

profile of v9, /device:TPU:1, one launch (start us, length us, event | category | flops | bytes accessed | tf_op | source)
XLA Modules:
  0.0 17.1 jit_solution(8582677934635137466)
XLA Ops:
  0.0 16.3 %shard_map.55 = (f32[3,3,128,128]{3,2,1,0:T(8,128)S(1)}, f32[1,128]{1,0:T(1,128)S(1)}) custom-call(s32[1,16]{1,0:T(1,128)} %bitcast.16, s32[2048,128]{1,0:T(8,128)} %bitcast.12, f32[16,16]{1,0:T(8,128)} %bitcast.14, f32[16,16]{1,0:T(8,128)} %bitcast.15, f32[3,16,16]{2,1,0:T(8,128)} %bitcast.13), custom_call_target="tpu_custom_call" | custom-call | tf_op jit(solution)/shard_map/pallas_call | solution.py:425
  16.3 0.8 %shard_map.56 = f32[1152,128]{1,0:T(8,128)} custom-call(f32[1152,128]{1,0:T(8,128)S(1)} %bitcast.11, f32[1,128]{1,0:T(1,128)S(1)} %get-tuple-element.8.scale_ref), custom_call_target="tpu_custom_call" | custom-call | tf_op jit(solution)/shard_map/pallas_call | solution.py:473

commit v10 on v9

--- a/solution.py
+++ b/solution.py
@@ -42,7 +42,7 @@
     live_hbm, inc_hbm, lame_hbm, shear_hbm, stretch_hbm,
     block_ref, scale_ref,
     live, inc, tail, lame, shear, stretch, alive, weight, number, place, params, send, recv, row, row_recv, hub_recv,
-    tail_sem, in_sem, send_sem, recv_sem, cast_sem, here, ready,
+    tail_sem, in_sem, send_sem, recv_sem, cast_sem, told,
 ):
     n_tiles = send.shape[0]
     my_x, my_y, my_z = lax.axis_index("gx"), lax.axis_index("gy"), lax.axis_index("gz")
@@ -175,6 +175,7 @@
         len(hubs) + EARLY - jnp.where(is_hub, 1, 0) - jnp.where(is_early, 1, 0),
     )
 
+    row_group = jnp.where(my_z < n_z // 2, 0, jnp.where(my_z < n_z // 2 + 2, 4, 3))
     for x, y, z in hubs:
         source = lax.rem(my_x - x + n_x, n_x) * n_y + lax.rem(my_y - y + n_y, n_y)
 
@@ -184,7 +185,7 @@
                 src_ref=row,
                 dst_ref=hub_recv.at[my_z * n_xy + source],
                 send_sem=send_sem.at[0],
-                recv_sem=recv_sem.at[jnp.where(my_z < n_z // 2, 0, 3)],
+                recv_sem=recv_sem.at[row_group],
                 device_id={"gx": x, "gy": y, "gz": z},
                 device_id_type=MESH,
             ).start()
@@ -193,7 +194,7 @@
 
     @pl.when(jnp.logical_not(is_lead))
     def _():
-        pl.semaphore_signal(here, inc=1, device_id={"gz": LEAD}, device_id_type=MESH)
+        pl.semaphore_signal(told, inc=1, device_id={"gz": LEAD}, device_id_type=MESH)
 
     for t in range(n_tiles):
         onehot = inc[t * TILE : (t + 1) * TILE, :].astype(F32).astype(BF16)
@@ -219,15 +220,15 @@
 
     @pl.when(is_lead)
     def _():
-        pl.semaphore_wait(here, n_z - 1)
+        pl.semaphore_wait(told, n_z - 1)
         for step in line_steps:
             pl.semaphore_signal(
-                ready, inc=1, device_id={"gz": (LEAD + step) % n_z}, device_id_type=MESH
+                told, inc=1, device_id={"gz": (LEAD + step) % n_z}, device_id_type=MESH
             )
 
     @pl.when(jnp.logical_not(is_lead))
     def _():
-        pl.semaphore_wait(ready, 1)
+        pl.semaphore_wait(told, 1)
 
     for z in range(EARLY, n_z):
         send_tile(z)
@@ -345,8 +346,11 @@
         half = n_xy * n_z // 2
         rows(hub_recv, half - 1, send_sem.at[0], recv_sem.at[0]).wait_recv()
         first_half = sum_rows(hub_recv, 0, half)
-        rows(hub_recv, half, send_sem.at[0], recv_sem.at[3]).wait_recv()
-        scale = (3.0 * TILE * n_xy * n_z) / (first_half + sum_rows(hub_recv, half, 2 * half))
+        late = half + 2 * n_xy
+        rows(hub_recv, 2 * half - late, send_sem.at[0], recv_sem.at[3]).wait_recv()
+        before = first_half + sum_rows(hub_recv, late, 2 * half)
+        rows(hub_recv, late - half, send_sem.at[0], recv_sem.at[4]).wait_recv()
+        scale = (3.0 * TILE * n_xy * n_z) / (before + sum_rows(hub_recv, half, late))
         scale_ref[...] = scale
         row_recv[...] = scale
         @pl.when(jnp.logical_not(is_at(0, 0, LEAD)))
@@ -402,16 +406,13 @@
     tiles.wait_send()
 
 
-def scale_kernel(block_ref, scale_ref, out_hbm, scaled, sems):
+def scale_kernel(block_ref, scale_ref, out_hbm, scaled, sem):
     scale = scale_ref[...]
-    copies = []
     for k in range(3):
         part = pl.ds(k * 3 * TILE, 3 * TILE)
         scaled[part, :] = block_ref[part, :] * scale
-        copies.append(pltpu.make_async_copy(scaled.at[part], out_hbm.at[part], sems.at[k]))
-        copies[k].start()
-    for copy in copies:
-        copy.wait()
+        pltpu.make_async_copy(scaled.at[part], out_hbm.at[part], sem).start()
+    pltpu.make_async_copy(scaled, out_hbm, sem).wait()
 
 
 def solution(mesh):
@@ -450,9 +451,8 @@
                 pltpu.SemaphoreType.DMA,
                 pltpu.SemaphoreType.DMA((9,)),
                 pltpu.SemaphoreType.DMA((3,)),
-                pltpu.SemaphoreType.DMA((4,)),
+                pltpu.SemaphoreType.DMA((5,)),
                 pltpu.SemaphoreType.DMA,
-                pltpu.SemaphoreType.REGULAR,
                 pltpu.SemaphoreType.REGULAR,
             ],
             compiler_params=pltpu.CompilerParams(
@@ -475,7 +475,7 @@
             out_shape=jax.ShapeDtypeStruct((9 * TILE, TILE), F32),
             in_specs=[vmem, vmem],
             out_specs=hbm,
-            scratch_shapes=[pltpu.VMEM((9 * TILE, TILE), F32), pltpu.SemaphoreType.DMA((3,))],
+            scratch_shapes=[pltpu.VMEM((9 * TILE, TILE), F32), pltpu.SemaphoreType.DMA],
             compiler_params=pltpu.CompilerParams(vmem_limit_bytes=24 << 20),
         )(block.reshape(9 * TILE, TILE), scale)
         block = block.reshape(3, 3, TILE, TILE)

time: 17.2 us -> 17.2 us (level)
  no operation moved by 1% of the time
where the time goes in v10:
time: 17.2 us; the launch traced here: 17.1 us
  Pallas kernels  17.1 us (99%)
    pallas_call x1, Pallas kernels, on_device(): pl.pallas_call(functools.partial(kernel, n_x, n_y, n_z), out_shape=(jax.S...  16.2 us
    pallas_call x1, Pallas kernels, on_device(): pl.pallas_call(scale_kernel, out_shape=jax.ShapeDtypeStruct((9 * TILE, TI...  0.83 us

profile of v10, /device:TPU:1, one launch (start us, length us, event | category | flops | bytes accessed | tf_op | source)
XLA Modules:
  0.0 17.1 jit_solution(13536386374762764730)
XLA Ops:
  0.0 16.2 %shard_map.55 = (f32[3,3,128,128]{3,2,1,0:T(8,128)S(1)}, f32[1,128]{1,0:T(1,128)S(1)}) custom-call(s32[1,16]{1,0:T(1,128)} %bitcast.16, s32[2048,128]{1,0:T(8,128)} %bitcast.12, f32[16,16]{1,0:T(8,128)} %bitcast.14, f32[16,16]{1,0:T(8,128)} %bitcast.15, f32[3,16,16]{2,1,0:T(8,128)} %bitcast.13), custom_call_target="tpu_custom_call" | custom-call | tf_op jit(solution)/shard_map/pallas_call | solution.py:426
  16.2 0.8 %shard_map.56 = f32[1152,128]{1,0:T(8,128)} custom-call(f32[1152,128]{1,0:T(8,128)S(1)} %bitcast.11, f32[1,128]{1,0:T(1,128)S(1)} %get-tuple-element.8.scale_ref), custom_call_target="tpu_custom_call" | custom-call | tf_op jit(solution)/shard_map/pallas_call | solution.py:473

commit v11 on v10

--- a/solution.py
+++ b/solution.py
@@ -208,7 +208,7 @@
             pltpu.make_async_remote_copy(
                 src_ref=send.at[z],
                 dst_ref=recv.at[lax.rem(my_z - z + n_z, n_z)],
-                send_sem=send_sem.at[1],
+                send_sem=send_sem.at[0],
                 recv_sem=recv_sem.at[1],
                 device_id={"gz": z},
                 device_id_type=MESH,
@@ -243,7 +243,7 @@
             device_id_type=MESH,
         )
 
-    tiles = rows(recv, n_z - 1, send_sem.at[1], recv_sem.at[1])
+    tiles = rows(recv, n_z - 1, send_sem.at[0], recv_sem.at[1])
     tiles.wait_recv()
 
     halves = range(n_z // 8)
@@ -395,15 +395,13 @@
                 def _():
                     rows(hub_recv, max(owned - 1, 0) * n_z + own, cast_sem, recv_sem.at[2]).wait_send()
 
-        rows(hub_recv, len(hubs) - 1, send_sem.at[0], recv_sem.at[0]).wait_send()
+        rows(hub_recv, 2 * (n_z - 1) + len(hubs) - 1, send_sem.at[0], recv_sem.at[0]).wait_send()
 
     @pl.when(jnp.logical_not(is_hub))
     def _():
-        rows(hub_recv, 1, send_sem.at[2], recv_sem.at[2]).wait_recv()
+        rows(hub_recv, 1, send_sem.at[0], recv_sem.at[2]).wait_recv()
         scale_ref[...] = row_recv[...]
-        rows(hub_recv, len(hubs), send_sem.at[0], recv_sem.at[0]).wait_send()
-
-    tiles.wait_send()
+        rows(hub_recv, 2 * (n_z - 1) + len(hubs), send_sem.at[0], recv_sem.at[0]).wait_send()
 
 
 def scale_kernel(block_ref, scale_ref, out_hbm, scaled, sem):
@@ -450,7 +448,7 @@
                 pltpu.VMEM((n_xy * n_z, 1, TILE), F32),
                 pltpu.SemaphoreType.DMA,
                 pltpu.SemaphoreType.DMA((9,)),
-                pltpu.SemaphoreType.DMA((3,)),
+                pltpu.SemaphoreType.DMA((1,)),
                 pltpu.SemaphoreType.DMA((5,)),
                 pltpu.SemaphoreType.DMA,
                 pltpu.SemaphoreType.REGULAR,

time: 17.2 us -> 17.2 us (level)
  no operation moved by 1% of the time
where the time goes in v11:
time: 17.2 us; the launch traced here: 17.1 us
  Pallas kernels  17.1 us (99%)
    pallas_call x1, Pallas kernels, on_device(): pl.pallas_call(functools.partial(kernel, n_x, n_y, n_z), out_shape=(jax.S...  16.2 us
    pallas_call x1, Pallas kernels, on_device(): pl.pallas_call(scale_kernel, out_shape=jax.ShapeDtypeStruct((9 * TILE, TI...  0.83 us

profile of v11, /device:TPU:1, one launch (start us, length us, event | category | flops | bytes accessed | tf_op | source)
XLA Modules:
  0.0 17.1 jit_solution(5391407691392845264)
XLA Ops:
  0.0 16.2 %shard_map.55 = (f32[3,3,128,128]{3,2,1,0:T(8,128)S(1)}, f32[1,128]{1,0:T(1,128)S(1)}) custom-call(s32[1,16]{1,0:T(1,128)} %bitcast.16, s32[2048,128]{1,0:T(8,128)} %bitcast.12, f32[16,16]{1,0:T(8,128)} %bitcast.14, f32[16,16]{1,0:T(8,128)} %bitcast.15, f32[3,16,16]{2,1,0:T(8,128)} %bitcast.13), custom_call_target="tpu_custom_call" | custom-call | tf_op jit(solution)/shard_map/pallas_call | solution.py:424
  16.2 0.8 %shard_map.56 = f32[1152,128]{1,0:T(8,128)} custom-call(f32[1152,128]{1,0:T(8,128)S(1)} %bitcast.11, f32[1,128]{1,0:T(1,128)S(1)} %get-tuple-element.8.scale_ref), custom_call_target="tpu_custom_call" | custom-call | tf_op jit(solution)/shard_map/pallas_call | solution.py:471
